TPU v7x, 32 devices: a whole 2x2x4 slice. The times are simulated.
32 devices in a mesh: seqs: 4 (over y, x), blk: 4 (over z), mp: 2 (over core).
Axes of the slice: x: 2, y: 2, z: 4, core: 2. Of those that a mesh axis runs over, the one named last changes fastest.
Arguments:
- block_input: float32 [2048, 1536], P(('seqs', 'blk')), may hold values from -6 to 6
- cotangent: float32 [2048, 1536], P(('seqs', 'blk')), may hold values from -6 to 6
- lengths: int32 [4], P('seqs'), may hold values from 128 to 512, as said below
- offsets: int32 [4], P('seqs'), may hold values from 2048 to 4095
- ssm_state: bfloat16 [4, 16, 3072], P('seqs', None, ('blk', 'mp')), may hold values from -6 to 6
- conv_state: bfloat16 [4, 3, 3072], P('seqs', None, ('blk', 'mp')), may hold values from -6 to 6
- kv_cache: bfloat16 [4, 2, 2048, 1536], P('seqs', None, 'blk', 'mp'), may hold values from -6 to 6
- norm_gains: bfloat16 [4, 1536], P(None, 'blk'), may hold values from 0.5 to 1.5
- w_in: bfloat16 [2, 1536, 3072], P(None, None, ('blk', 'mp')), may hold values from -0.15625 to 0.15625
- conv_weight: bfloat16 [4, 3072], P(None, ('blk', 'mp')), may hold values from -3 to 3
- conv_bias: bfloat16 [3072], P(('blk', 'mp')), may hold values from -3 to 3
- x_proj: bfloat16 [128, 3072], P(None, ('blk', 'mp')), may hold values from -0.109375 to 0.109375
- dt_proj: bfloat16 [96, 3072], P(None, ('blk', 'mp')), may hold values from -0.625 to 0.625
- dt_bias: bfloat16 [3072], P(('blk', 'mp')), may hold values from -5 to -3
- a_log: bfloat16 [16, 3072], P(None, ('blk', 'mp'))
- d_skip: bfloat16 [3072], P(('blk', 'mp')), may hold values from 0.5 to 1.5
- mamba_out: bfloat16 [3072, 1536], P(('blk', 'mp')), may hold values from -0.109375 to 0.109375
- ffn1_gate_up: bfloat16 [2, 1536, 4096], P(None, None, ('blk', 'mp')), may hold values from -0.15625 to 0.15625
- ffn1_down: bfloat16 [4096, 1536], P(('blk', 'mp')), may hold values from -0.09375 to 0.09375
- qkv_proj: bfloat16 [3, 1536, 1536], P(None, 'blk', 'mp'), may hold values from -0.15625 to 0.15625
- attn_out: bfloat16 [1536, 1536], P('mp', 'blk'), may hold values from -3.5 to 3.5
- ffn2_gate_up: bfloat16 [2, 1536, 4096], P(None, None, ('blk', 'mp')), may hold values from -0.15625 to 0.15625
- ffn2_down: bfloat16 [4096, 1536], P(('blk', 'mp')), may hold values from -0.09375 to 0.09375
Outputs:
- block_output: float32 [2048, 1536], P(('seqs', 'blk'))
- input_grad: float32 [2048, 1536], P(('seqs', 'blk'))
- new_ssm_state: bfloat16 [4, 16, 3072], P('seqs', None, ('blk', 'mp'))
- new_conv_state: bfloat16 [4, 3, 3072], P('seqs', None, ('blk', 'mp'))
- new_kv_cache: bfloat16 [4, 2, 2048, 1536], P('seqs', None, 'blk', 'mp')
- ssm_state_grad: float32 [4, 16, 3072], P('seqs', None, ('blk', 'mp'))
- conv_state_grad: float32 [4, 3, 3072], P('seqs', None, ('blk', 'mp'))
- kv_cache_grad: float32 [4, 2, 2048, 1536], P('seqs', None, 'blk', 'mp')
- norm_gains_grad: float32 [4, 1536], P(None, 'blk')
- w_in_grad: float32 [2, 1536, 3072], P(None, None, ('blk', 'mp'))
- conv_weight_grad: float32 [4, 3072], P(None, ('blk', 'mp'))
- conv_bias_grad: float32 [3072], P(('blk', 'mp'))
- x_proj_grad: float32 [128, 3072], P(None, ('blk', 'mp'))
- dt_proj_grad: float32 [96, 3072], P(None, ('blk', 'mp'))
- dt_bias_grad: float32 [3072], P(('blk', 'mp'))
- a_log_grad: float32 [16, 3072], P(None, ('blk', 'mp'))
- d_skip_grad: float32 [3072], P(('blk', 'mp'))
- mamba_out_grad: float32 [3072, 1536], P(('blk', 'mp'))
- ffn1_gate_up_grad: float32 [2, 1536, 4096], P(None, None, ('blk', 'mp'))
- ffn1_down_grad: float32 [4096, 1536], P(('blk', 'mp'))
- qkv_proj_grad: float32 [3, 1536, 1536], P(None, 'blk', 'mp')
- attn_out_grad: float32 [1536, 1536], P('mp', 'blk')
- ffn2_gate_up_grad: float32 [2, 1536, 4096], P(None, None, ('blk', 'mp'))
- ffn2_down_grad: float32 [4096, 1536], P(('blk', 'mp'))
Inputs may be any that keep to these rules, and one draw needn't show every extreme that they name: `lengths`: one sequence has exactly 512 tokens and one exactly 128; the others lie between.
All inputs are finite; a program needn't handle non-finite values.
Results may differ from a plain program's by a relative error of at most 0.039.
Values may be sent and summed in bfloat16 or wider, within the bound.
No kernel may reach another device: no remote copies, remote signals or barrier semaphores. Data moves between devices by JAX's collectives and lax.ppermute only.
A program may use at most 512 MiB of HBM per device.

v0:
```python
import jax
import jax.numpy as jnp
from jax import lax
from jax.sharding import PartitionSpec as P

HD = 128


EPSILON = 1e-05
ROPE_BASE = 10000.0
NEG_BIG = -1e30


def passed_along(value, axis, steps):
    count = lax.axis_size(axis)
    leading, last = (max(0, -steps), min(count, count - steps))
    return lax.ppermute(value, axis, [(source, source + steps) for source in range(leading, last)])


def matmul(left_op, right_op):
    return jnp.dot(left_op, right_op, preferred_element_type=jnp.float32)


def matmul_tn(left_op, right_op):
    return lax.dot_general(
        left_op, right_op, (((0,), (0,)), ((), ())), preferred_element_type=jnp.float32
    )


def matmul_nt(left_op, right_op):
    return lax.dot_general(
        left_op, right_op, (((1,), (1,)), ((), ())), preferred_element_type=jnp.float32
    )


def model_sum(partial_sum):
    return lax.psum(partial_sum.astype(jnp.bfloat16), "mp").astype(jnp.float32)


def conv_shift(edge_rows, step_by):
    return passed_along(edge_rows, "blk", step_by)


def norm_forward(values, norm_gain):
    inverse = lax.rsqrt(jnp.mean(values * values, axis=-1, keepdims=True) + EPSILON)
    unit_rows = values * inverse
    return (unit_rows * norm_gain, unit_rows, inverse)


def norm_backward(grad_out, unit_rows, inverse, norm_gain):
    grad_unit = grad_out * norm_gain
    grad_gain = jnp.sum(grad_out * unit_rows, axis=0)
    grad_in = inverse * (
        grad_unit - unit_rows * jnp.mean(grad_unit * unit_rows, axis=-1, keepdims=True)
    )
    return (grad_in, grad_gain)


def silu_slope(values):
    logistic = jax.nn.sigmoid(values)
    return logistic * (1.0 + values * (1.0 - logistic))


def rotation_tables(positions):
    half_dim = HD // 2
    frequency = ROPE_BASE ** (-(jnp.arange(half_dim, dtype=jnp.float32) * 2.0 / HD))
    angles = positions.astype(jnp.float32)[:, None] * frequency[None, :]
    return (jnp.cos(angles), jnp.sin(angles))


def rotate(values, cosine, sine_part, direction):
    count_rows = values.shape[0]
    by_head = values.reshape(count_rows, -1, HD)
    half_dim = HD // 2
    cos_rows = cosine[:, None, :]
    sin_rows = direction * sine_part[:, None, :]
    first_half = by_head[..., :half_dim]
    second_half = by_head[..., half_dim:]
    turned = jnp.concatenate(
        [
            first_half * cos_rows - second_half * sin_rows,
            second_half * cos_rows + first_half * sin_rows,
        ],
        axis=-1,
    )
    return turned.reshape(count_rows, -1)


def pair_combine(earlier, latter):
    return (earlier[0] * latter[0], latter[0] * earlier[1] + latter[1])


def scan_piece(entering, step_size, in_coef, out_coef, conv_out, decay_rate):
    tok_rows, channels = step_size.shape
    state_count = decay_rate.shape[0]
    piece_rows = min(8, tok_rows)
    groups = tok_rows // piece_rows
    step_grouped = step_size.reshape(groups, piece_rows, 1, channels)
    exponent = decay_rate[None, None] * jnp.cumsum(step_grouped, axis=1)
    shrink = jnp.exp(exponent)
    drive_in = in_coef.reshape(groups, piece_rows, state_count, 1) * (step_size * conv_out).reshape(
        groups, piece_rows, 1, channels
    )
    inner_state = shrink * jnp.cumsum(jnp.exp(-exponent) * drive_in, axis=1)
    total_decay, total_state = lax.associative_scan(
        pair_combine, (shrink[:, -1], inner_state[:, -1])
    )
    start_states = jnp.concatenate(
        [entering[None], total_decay[:-1] * entering[None] + total_state[:-1]], axis=0
    )
    states = shrink * start_states[:, None] + inner_state
    outputs = jnp.sum(
        out_coef.reshape(groups, piece_rows, state_count, 1) * states, axis=2
    ).reshape(tok_rows, channels)
    return (states[-1, -1], outputs)


def scan_tokens(entering, step_size, in_coef, out_coef, conv_out, decay_rate):
    tok_rows, channels = step_size.shape
    chan_width = min(512, channels)
    block_count = channels // chan_width

    def by_block(array_in):
        return array_in.reshape(array_in.shape[0], block_count, chan_width).transpose(1, 0, 2)

    checked = jax.checkpoint(scan_piece)

    def one_block(block_args):
        return checked(
            block_args[0], block_args[1], in_coef, out_coef, block_args[2], block_args[3]
        )

    leaving, outputs = lax.map(
        one_block,
        (by_block(entering), by_block(step_size), by_block(conv_out), by_block(decay_rate)),
    )
    leaving = leaving.transpose(1, 0, 2).reshape(entering.shape[0], channels)
    outputs = outputs.transpose(1, 0, 2).reshape(tok_rows, channels)
    return (leaving, outputs)


def tail_rows(pieces, first_pos, seq_len, tail_len, along):
    row_count = pieces.shape[along]
    pad_shape = list(pieces.shape)
    pad_shape[along] = tail_len
    filler = jnp.zeros(pad_shape, pieces.dtype)
    buffer = jnp.concatenate([filler, pieces, filler], axis=along)
    begin_at = jnp.clip(seq_len - first_pos, 0, row_count + tail_len)
    return lax.dynamic_slice_in_dim(buffer, begin_at, tail_len, along)


def chain(decay, local_part, seed, backward):
    dev_count = lax.axis_size("blk")
    dev_index = lax.axis_index("blk")
    first_dev = dev_index == (dev_count - 1 if backward else 0)
    step_by = -1 if backward else 1

    def one_hop(hop_turn, entering):
        arrived = passed_along(
            (decay * entering + local_part).astype(jnp.bfloat16), "blk", step_by
        ).astype(jnp.float32)
        return jnp.where(first_dev, seed, arrived)

    return lax.fori_loop(0, dev_count - 1, one_hop, seed)


def mamba_forward(
    resid, norm_gain, mamba_weights, seed_state, seed_rows, is_valid, first_pos, seq_len
):
    w_in_l, conv_w_l, conv_b_l, x_proj_l, dt_proj_l, dt_bias_l, a_log_l, d_skip_l, out_l = (
        mamba_weights
    )
    tok_rows = resid.shape[0]
    tap_count = conv_w_l.shape[0]
    dev_index = lax.axis_index("blk")
    normed, unit_rows, inverse = norm_forward(resid, norm_gain)
    normed_low = normed.astype(jnp.bfloat16)
    x_lin = matmul(normed_low, w_in_l[0])
    z_lin = matmul(normed_low, w_in_l[1])
    x_low = x_lin.astype(jnp.bfloat16)
    arrived = conv_shift(x_low[tok_rows - (tap_count - 1) :].astype(jnp.float32), 1)
    before = jnp.where(dev_index == 0, seed_rows, arrived).astype(jnp.bfloat16)
    padded = jnp.concatenate([before, x_low], axis=0)
    conv_weight_f = conv_w_l.astype(jnp.float32)
    conv_pre = conv_b_l.astype(jnp.float32) + sum(
        (conv_weight_f[tap_at] * padded[tap_at : tap_at + tok_rows] for tap_at in range(tap_count))
    )
    conv_out = jax.nn.silu(conv_pre)
    conv_low = conv_out.astype(jnp.bfloat16)
    projected = model_sum(matmul_nt(conv_low, x_proj_l))
    dt_rank = dt_proj_l.shape[0]
    state_count = a_log_l.shape[0]
    dt_low = projected[:, :dt_rank].astype(jnp.bfloat16)
    in_coef = projected[:, dt_rank : dt_rank + state_count]
    out_coef = projected[:, dt_rank + state_count :]
    dt_lin = matmul(dt_low, dt_proj_l) + dt_bias_l.astype(jnp.float32)
    step_size = jax.nn.softplus(dt_lin) * is_valid
    decay_rate = -jnp.exp(a_log_l.astype(jnp.float32))
    cumulative = jnp.cumsum(step_size, axis=0)
    total_step = cumulative[-1]
    decay_total = jnp.exp(decay_rate * total_step[None, :])
    remaining = jnp.exp(decay_rate[None, :, :] * (total_step[None, :] - cumulative)[:, None, :])
    drive_in = step_size * conv_out
    local_state = jnp.sum(remaining * in_coef[:, :, None] * drive_in[:, None, :], axis=0)
    entering = chain(decay_total, local_state, seed_state, False)
    (leaving, scanned), pull_back = jax.vjp(
        scan_tokens, entering, step_size, in_coef, out_coef, conv_out, decay_rate
    )
    mixed_out = scanned + d_skip_l.astype(jnp.float32) * conv_out
    gated_low = (mixed_out * jax.nn.silu(z_lin)).astype(jnp.bfloat16)
    after_mix = resid + is_valid * model_sum(matmul(gated_low, out_l))
    tail_conv = tail_rows(x_low, first_pos, seq_len, tap_count - 1, 0).astype(jnp.float32)
    final_state = jnp.where(dev_index == lax.axis_size("blk") - 1, leaving, 0.0)
    kept_vals = (
        normed_low,
        unit_rows,
        inverse,
        z_lin,
        padded,
        conv_pre,
        conv_out,
        conv_low,
        dt_low,
        dt_lin,
        out_coef,
        cumulative,
        decay_rate,
        decay_total,
        pull_back,
        mixed_out,
        gated_low,
    )
    return (after_mix, kept_vals, final_state, tail_conv)


def mamba_backward(grad_after, kept_vals, norm_gain, mamba_weights, is_valid):
    w_in_l, conv_w_l, x_proj_l, dt_proj_l, d_skip_l, out_l = mamba_weights
    (
        normed_low,
        unit_rows,
        inverse,
        z_lin,
        padded,
        conv_pre,
        conv_out,
        conv_low,
        dt_low,
        dt_lin,
        out_coef,
        cumulative,
        decay_rate,
        decay_total,
        pull_back,
        mixed_out,
        gated_low,
    ) = kept_vals
    tok_rows = grad_after.shape[0]
    tap_count = conv_w_l.shape[0]
    dev_index = lax.axis_index("blk")
    grad_branch = (is_valid * grad_after).astype(jnp.bfloat16)
    grad_out_w = matmul_tn(gated_low, grad_branch)
    grad_gated = matmul_nt(grad_branch, out_l)
    grad_mixed = grad_gated * jax.nn.silu(z_lin)
    grad_z = grad_gated * mixed_out * silu_slope(z_lin)
    grad_skip = jnp.sum(grad_mixed * conv_out, axis=0)
    growth = jnp.exp(decay_rate[None, :, :] * cumulative[:, None, :])
    local_adj = jnp.sum(growth * out_coef[:, :, None] * grad_mixed[:, None, :], axis=0)
    grad_leaving = chain(decay_total, local_adj, jnp.zeros_like(local_adj), True)
    grad_entering, grad_step, grad_in_coef, grad_out_coef, grad_conv_scan, grad_decay = pull_back(
        (grad_leaving, grad_mixed)
    )
    grad_dt_low = (grad_step * is_valid * jax.nn.sigmoid(dt_lin)).astype(jnp.bfloat16)
    grad_dt_bias = jnp.sum(grad_dt_low.astype(jnp.float32), axis=0)
    grad_dt_proj = matmul_tn(dt_low, grad_dt_low)
    grad_proj_low = model_sum(
        jnp.concatenate([matmul_nt(grad_dt_low, dt_proj_l), grad_in_coef, grad_out_coef], axis=1)
    ).astype(jnp.bfloat16)
    grad_x_proj = matmul_tn(grad_proj_low, conv_low)
    grad_conv_out = (
        grad_conv_scan + grad_mixed * d_skip_l.astype(jnp.float32) + matmul(grad_proj_low, x_proj_l)
    )
    grad_pre = grad_conv_out * silu_slope(conv_pre)
    grad_conv_b = jnp.sum(grad_pre, axis=0)
    conv_weight_f = conv_w_l.astype(jnp.float32)
    grad_conv_w = jnp.stack(
        [
            jnp.sum(grad_pre * padded[tap_at : tap_at + tok_rows], axis=0)
            for tap_at in range(tap_count)
        ]
    )
    grad_padded = sum(
        (
            jnp.pad(conv_weight_f[tap_at] * grad_pre, ((tap_at, tap_count - 1 - tap_at), (0, 0)))
            for tap_at in range(tap_count)
        )
    )
    grad_before = grad_padded[: tap_count - 1]
    returned = conv_shift(grad_before, -1)
    grad_x = grad_padded[tap_count - 1 :] + jnp.pad(
        returned, ((tok_rows - (tap_count - 1), 0), (0, 0))
    )
    grad_seed_rows = jnp.where(dev_index == 0, grad_before, 0.0)
    grad_seed_state = jnp.where(dev_index == 0, grad_entering, 0.0)
    grad_xz_low = jnp.stack([grad_x, grad_z]).astype(jnp.bfloat16)
    grad_w_in = jnp.stack(
        [matmul_tn(normed_low, grad_xz_low[0]), matmul_tn(normed_low, grad_xz_low[1])]
    )
    grad_normed = model_sum(
        jnp.einsum("ktc,kdc->td", grad_xz_low, w_in_l, preferred_element_type=jnp.float32)
    )
    grad_in, grad_gain = norm_backward(grad_normed, unit_rows, inverse, norm_gain)
    grad_a_log = grad_decay * decay_rate
    mamba_grads = (
        grad_w_in,
        grad_conv_w,
        grad_conv_b,
        grad_x_proj,
        grad_dt_proj,
        grad_dt_bias,
        grad_a_log,
        grad_skip,
        grad_out_w,
    )
    return (grad_after + grad_in, grad_gain, mamba_grads, grad_seed_state, grad_seed_rows)


def ffn_forward(resid, norm_gain, gate_up_l, down_l, is_valid):
    normed, unit_rows, inverse = norm_forward(resid, norm_gain)
    normed_low = normed.astype(jnp.bfloat16)
    gate_lin = matmul(normed_low, gate_up_l[0])
    up_lin = matmul(normed_low, gate_up_l[1])
    hidden_low = (jax.nn.silu(gate_lin) * up_lin).astype(jnp.bfloat16)
    after_mix = resid + is_valid * model_sum(matmul(hidden_low, down_l))
    return (after_mix, (normed_low, unit_rows, inverse, gate_lin, up_lin, hidden_low))


def ffn_backward(grad_after, kept_vals, norm_gain, gate_up_l, down_l, is_valid):
    normed_low, unit_rows, inverse, gate_lin, up_lin, hidden_low = kept_vals
    grad_branch = (is_valid * grad_after).astype(jnp.bfloat16)
    grad_down = matmul_tn(hidden_low, grad_branch)
    grad_hidden = matmul_nt(grad_branch, down_l)
    grad_gate = grad_hidden * up_lin * silu_slope(gate_lin)
    grad_up = grad_hidden * jax.nn.silu(gate_lin)
    grad_gu_low = jnp.stack([grad_gate, grad_up]).astype(jnp.bfloat16)
    grad_gate_up = jnp.stack(
        [matmul_tn(normed_low, grad_gu_low[0]), matmul_tn(normed_low, grad_gu_low[1])]
    )
    grad_normed = model_sum(
        jnp.einsum("ktc,kdc->td", grad_gu_low, gate_up_l, preferred_element_type=jnp.float32)
    )
    grad_in, grad_gain = norm_backward(grad_normed, unit_rows, inverse, norm_gain)
    return (grad_after + grad_in, grad_gain, grad_gate_up, grad_down)


def window_mask(tok_rows, key_count, window, first_pos, seq_len):
    query_at = jnp.arange(tok_rows, dtype=jnp.int32)[:, None]
    key_at = jnp.arange(key_count, dtype=jnp.int32)[None, :]
    return (
        (key_at > query_at)
        & (key_at <= query_at + window)
        & (key_at < seq_len - first_pos + window)
    )


def window_scores(q_low, all_kv, in_window):
    heads_l = q_low.shape[1] // HD
    q_heads = q_low.reshape(q_low.shape[0], heads_l, HD)
    k_heads = all_kv[0].reshape(all_kv.shape[1], heads_l, HD)
    scores = jnp.einsum(
        "qhd,khd->hqk", q_heads, k_heads, preferred_element_type=jnp.float32
    ) * HD ** (-0.5)
    return jnp.where(in_window[None], scores, NEG_BIG)


def attention_forward(
    resid, norm_gain, qkv_l, out_l, cache_full, cosine, sine_part, is_valid, first_pos, seq_len
):
    tok_rows = resid.shape[0]
    window = cache_full.shape[1]
    reach_blocks = window // tok_rows
    dev_index = lax.axis_index("blk")
    dev_count = lax.axis_size("blk")
    normed, unit_rows, inverse = norm_forward(resid, norm_gain)
    normed_low = normed.astype(jnp.bfloat16)
    q_low = rotate(matmul(normed_low, qkv_l[0]), cosine, sine_part, 1.0).astype(jnp.bfloat16)
    k_low = rotate(matmul(normed_low, qkv_l[1]), cosine, sine_part, 1.0).astype(jnp.bfloat16)
    v_low = matmul(normed_low, qkv_l[2]).astype(jnp.bfloat16)
    local_kv = jnp.stack([k_low, v_low])
    cache_pad = jnp.concatenate([cache_full, jnp.zeros_like(cache_full)], axis=1)
    window_kv = lax.dynamic_slice_in_dim(cache_pad, first_pos, window, 1)
    hop_count = min(reach_blocks, dev_count - 1)

    def hop_step(hop_turn, carried):
        travel, window_now = carried
        travel = passed_along(travel, "blk", 1)
        distance = hop_turn + 1
        slot_start = (reach_blocks - distance) * tok_rows
        current = lax.dynamic_slice_in_dim(window_now, slot_start, tok_rows, 1)
        chosen = jnp.where(dev_index >= distance, travel, current)
        return (travel, lax.dynamic_update_slice_in_dim(window_now, chosen, slot_start, 1))

    _, window_kv = lax.fori_loop(0, hop_count, hop_step, (local_kv, window_kv))
    all_kv = jnp.concatenate([window_kv, local_kv], axis=1)
    key_count = all_kv.shape[1]
    in_window = window_mask(tok_rows, key_count, window, first_pos, seq_len)
    masked = window_scores(q_low, all_kv, in_window)
    row_max = jnp.max(masked, axis=-1, keepdims=True)
    exp_rows = jnp.exp(masked - row_max)
    row_total = jnp.sum(exp_rows, axis=-1, keepdims=True)
    attn_prob = exp_rows / row_total
    log_total = row_max + jnp.log(row_total)
    heads_l = q_low.shape[1] // HD
    v_heads = all_kv[1].reshape(key_count, heads_l, HD)
    attended = jnp.einsum(
        "hqk,khd->qhd", attn_prob.astype(jnp.bfloat16), v_heads, preferred_element_type=jnp.float32
    )
    att_low = attended.reshape(tok_rows, heads_l * HD).astype(jnp.bfloat16)
    after_mix = resid + is_valid * model_sum(matmul(att_low, out_l))
    tail_index = jnp.arange(window, dtype=jnp.int32)
    from_cache = lax.dynamic_slice_in_dim(cache_pad, jnp.minimum(seq_len, window), window, 1)
    use_cache = (tail_index < window - seq_len) & (dev_index == 0)
    tail_cache = tail_rows(local_kv, first_pos, seq_len, window, 1).astype(jnp.float32) + jnp.where(
        use_cache[None, :, None], from_cache.astype(jnp.float32), 0.0
    )
    kept_vals = (normed_low, unit_rows, inverse, q_low, all_kv, log_total, att_low, in_window)
    return (after_mix, kept_vals, tail_cache)


def attention_backward(grad_after, kept_vals, norm_gain, qkv_l, out_l, cosine, sine_part, is_valid):
    normed_low, unit_rows, inverse, q_low, all_kv, log_total, att_low, in_window = kept_vals
    tok_rows = grad_after.shape[0]
    key_count = all_kv.shape[1]
    window = key_count - tok_rows
    reach_blocks = window // tok_rows
    dev_index = lax.axis_index("blk")
    dev_count = lax.axis_size("blk")
    heads_l = q_low.shape[1] // HD
    width_l = heads_l * HD
    score_scale = HD ** (-0.5)
    grad_branch = (is_valid * grad_after).astype(jnp.bfloat16)
    grad_wo = matmul_tn(att_low, grad_branch)
    grad_att = matmul_nt(grad_branch, out_l).astype(jnp.bfloat16).reshape(tok_rows, heads_l, HD)
    masked = window_scores(q_low, all_kv, in_window)
    attn_prob = jnp.exp(masked - log_total)
    probs_low = attn_prob.astype(jnp.bfloat16)
    q_heads = q_low.reshape(tok_rows, heads_l, HD)
    k_heads = all_kv[0].reshape(key_count, heads_l, HD)
    v_heads = all_kv[1].reshape(key_count, heads_l, HD)
    grad_prob = jnp.einsum("qhd,khd->hqk", grad_att, v_heads, preferred_element_type=jnp.float32)
    row_delta = jnp.sum(grad_prob * attn_prob, axis=-1, keepdims=True)
    grad_scores = (attn_prob * (grad_prob - row_delta)).astype(jnp.bfloat16)
    grad_q = (
        jnp.einsum("hqk,khd->qhd", grad_scores, k_heads, preferred_element_type=jnp.float32)
        * score_scale
    )
    grad_k_all = (
        jnp.einsum("hqk,qhd->khd", grad_scores, q_heads, preferred_element_type=jnp.float32)
        * score_scale
    )
    grad_v_all = jnp.einsum("hqk,qhd->khd", probs_low, grad_att, preferred_element_type=jnp.float32)
    grad_kv_all = jnp.stack(
        [grad_k_all.reshape(key_count, width_l), grad_v_all.reshape(key_count, width_l)]
    )
    cache_mask = jnp.arange(window, dtype=jnp.int32) < window - dev_index * tok_rows
    cache_part = jnp.where(cache_mask[None, :, None], grad_kv_all[:, :window], 0.0)
    cache_grad = lax.dynamic_update_slice_in_dim(
        jnp.zeros((2, 2 * window, width_l), jnp.float32), cache_part, dev_index * tok_rows, 1
    )[:, :window]
    hop_count = min(reach_blocks, dev_count - 1)

    def cycle_part(distance):
        piece_rows = lax.dynamic_slice_in_dim(
            grad_kv_all, (reach_blocks - distance) * tok_rows, tok_rows, 1
        )
        return jnp.where((dev_index >= distance) & (distance >= 1), piece_rows, 0.0)

    def back_step(hop_turn, carried_adj):
        return passed_along(carried_adj.astype(jnp.bfloat16), "blk", -1).astype(
            carried_adj.dtype
        ) + cycle_part(hop_count - 1 - hop_turn)

    carried_adj = lax.fori_loop(0, hop_count, back_step, cycle_part(hop_count))
    grad_local = grad_kv_all[:, window:] + carried_adj
    grad_q_lin = rotate(grad_q.reshape(tok_rows, width_l), cosine, sine_part, -1.0)
    grad_k_lin = rotate(grad_local[0], cosine, sine_part, -1.0)
    grad_qkv_low = jnp.stack([grad_q_lin, grad_k_lin, grad_local[1]]).astype(jnp.bfloat16)
    grad_qkv = jnp.stack([matmul_tn(normed_low, grad_qkv_low[member]) for member in range(3)])
    grad_normed = model_sum(
        jnp.einsum("ktc,kdc->td", grad_qkv_low, qkv_l, preferred_element_type=jnp.float32)
    )
    grad_in, grad_gain = norm_backward(grad_normed, unit_rows, inverse, norm_gain)
    return (grad_after + grad_in, grad_gain, grad_qkv, grad_wo, cache_grad)


def shards(
    block_input,
    cotangent,
    lengths,
    offsets,
    ssm_state,
    conv_state,
    kv_cache,
    norm_gains,
    w_in,
    conv_weight,
    conv_bias,
    x_proj,
    dt_proj,
    dt_bias,
    a_log,
    d_skip,
    mamba_out,
    ffn1_gate_up,
    ffn1_down,
    qkv_proj,
    attn_out,
    ffn2_gate_up,
    ffn2_down,
):
    (
        ssm_full,
        conv_full,
        cache_full,
        gains_full,
        w_in_full,
        conv_w_full,
        conv_b_full,
        x_proj_full,
        dt_proj_full,
        dt_bias_full,
        a_log_full,
        d_skip_full,
        mamba_out_full,
        gate_up_one,
        down_one,
        qkv_full,
        attn_out_full,
        gate_up_two,
        down_two,
    ) = (
        lax.all_gather(ssm_state, "blk", axis=2, tiled=True),
        lax.all_gather(conv_state, "blk", axis=2, tiled=True),
        lax.all_gather(kv_cache, "blk", axis=2, tiled=True),
        lax.all_gather(norm_gains, "blk", axis=1, tiled=True),
        lax.all_gather(w_in, "blk", axis=2, tiled=True),
        lax.all_gather(conv_weight, "blk", axis=1, tiled=True),
        lax.all_gather(conv_bias, "blk", axis=0, tiled=True),
        lax.all_gather(x_proj, "blk", axis=1, tiled=True),
        lax.all_gather(dt_proj, "blk", axis=1, tiled=True),
        lax.all_gather(dt_bias, "blk", axis=0, tiled=True),
        lax.all_gather(a_log, "blk", axis=1, tiled=True),
        lax.all_gather(d_skip, "blk", axis=0, tiled=True),
        lax.all_gather(mamba_out, "blk", axis=0, tiled=True),
        lax.all_gather(ffn1_gate_up, "blk", axis=2, tiled=True),
        lax.all_gather(ffn1_down, "blk", axis=0, tiled=True),
        lax.all_gather(qkv_proj, "blk", axis=1, tiled=True),
        lax.all_gather(attn_out, "blk", axis=1, tiled=True),
        lax.all_gather(ffn2_gate_up, "blk", axis=2, tiled=True),
        lax.all_gather(ffn2_down, "blk", axis=0, tiled=True),
    )
    tok_rows = block_input.shape[0]
    dev_index = lax.axis_index("blk")
    first_pos = dev_index * tok_rows
    seq_len = lengths[0]
    row_pos = first_pos + jnp.arange(tok_rows, dtype=jnp.int32)
    is_valid = (row_pos < seq_len).astype(jnp.float32)[:, None]
    cosine, sine_part = rotation_tables(offsets[0] + row_pos)
    gain_rows = gains_full.astype(jnp.float32)
    after_mamba, kept_mamba, final_state, tail_conv = mamba_forward(
        block_input,
        gain_rows[0],
        (
            w_in_full,
            conv_w_full,
            conv_b_full,
            x_proj_full,
            dt_proj_full,
            dt_bias_full,
            a_log_full,
            d_skip_full,
            mamba_out_full,
        ),
        ssm_full[0].astype(jnp.float32),
        conv_full[0].astype(jnp.float32),
        is_valid,
        first_pos,
        seq_len,
    )
    after_ffn_one, kept_one = ffn_forward(
        after_mamba, gain_rows[1], gate_up_one, down_one, is_valid
    )
    after_attn, kept_attn, tail_cache = attention_forward(
        after_ffn_one,
        gain_rows[2],
        qkv_full,
        attn_out_full,
        cache_full[0],
        cosine,
        sine_part,
        is_valid,
        first_pos,
        seq_len,
    )
    block_output, kept_two = ffn_forward(after_attn, gain_rows[3], gate_up_two, down_two, is_valid)
    (
        w_in_back,
        conv_w_back,
        x_proj_back,
        dt_proj_back,
        d_skip_back,
        mamba_out_back,
        gate_up_one_back,
        down_one_back,
        qkv_back,
        attn_out_back,
        gate_up_two_back,
        down_two_back,
    ) = (
        lax.all_gather(w_in, "blk", axis=2, tiled=True),
        lax.all_gather(conv_weight, "blk", axis=1, tiled=True),
        lax.all_gather(x_proj, "blk", axis=1, tiled=True),
        lax.all_gather(dt_proj, "blk", axis=1, tiled=True),
        lax.all_gather(d_skip, "blk", axis=0, tiled=True),
        lax.all_gather(mamba_out, "blk", axis=0, tiled=True),
        lax.all_gather(ffn1_gate_up, "blk", axis=2, tiled=True),
        lax.all_gather(ffn1_down, "blk", axis=0, tiled=True),
        lax.all_gather(qkv_proj, "blk", axis=1, tiled=True),
        lax.all_gather(attn_out, "blk", axis=1, tiled=True),
        lax.all_gather(ffn2_gate_up, "blk", axis=2, tiled=True),
        lax.all_gather(ffn2_down, "blk", axis=0, tiled=True),
    )
    grad_now = cotangent
    grad_now, gain_grad_four, grad_gate_up_two, grad_down_two = ffn_backward(
        grad_now, kept_two, gain_rows[3], gate_up_two_back, down_two_back, is_valid
    )
    red_gate_up_two, red_down_two = (
        lax.psum_scatter(
            grad_gate_up_two.astype(jnp.bfloat16), "blk", scatter_dimension=2, tiled=True
        ).astype(jnp.float32),
        lax.psum_scatter(
            grad_down_two.astype(jnp.bfloat16), "blk", scatter_dimension=0, tiled=True
        ).astype(jnp.float32),
    )
    grad_now, gain_grad_three, grad_qkv, grad_wo, cache_grad = attention_backward(
        grad_now, kept_attn, gain_rows[2], qkv_back, attn_out_back, cosine, sine_part, is_valid
    )
    red_qkv, red_wo, red_tail_cache, red_cache_grad = (
        lax.psum_scatter(
            grad_qkv.astype(jnp.bfloat16), "blk", scatter_dimension=1, tiled=True
        ).astype(jnp.float32),
        lax.psum_scatter(
            grad_wo.astype(jnp.bfloat16), "blk", scatter_dimension=1, tiled=True
        ).astype(jnp.float32),
        lax.psum_scatter(
            tail_cache[None].astype(jnp.bfloat16), "blk", scatter_dimension=2, tiled=True
        ).astype(jnp.float32),
        lax.psum_scatter(
            cache_grad[None].astype(jnp.bfloat16), "blk", scatter_dimension=2, tiled=True
        ).astype(jnp.float32),
    )
    grad_now, gain_grad_two, grad_gate_up_one, grad_down_one = ffn_backward(
        grad_now, kept_one, gain_rows[1], gate_up_one_back, down_one_back, is_valid
    )
    red_gate_up_one, red_down_one = (
        lax.psum_scatter(
            grad_gate_up_one.astype(jnp.bfloat16), "blk", scatter_dimension=2, tiled=True
        ).astype(jnp.float32),
        lax.psum_scatter(
            grad_down_one.astype(jnp.bfloat16), "blk", scatter_dimension=0, tiled=True
        ).astype(jnp.float32),
    )
    grad_now, gain_grad_one, mamba_grads, grad_seed_state, grad_seed_rows = mamba_backward(
        grad_now,
        kept_mamba,
        gain_rows[0],
        (w_in_back, conv_w_back, x_proj_back, dt_proj_back, d_skip_back, mamba_out_back),
        is_valid,
    )
    (
        grad_w_in,
        grad_conv_w,
        grad_conv_b,
        grad_x_proj,
        grad_dt_proj,
        grad_dt_bias,
        grad_a_log,
        grad_skip,
        grad_out_w,
    ) = mamba_grads
    gain_grads = jnp.stack([gain_grad_one, gain_grad_two, gain_grad_three, gain_grad_four])
    (
        red_gains,
        red_w_in,
        red_conv_w,
        red_conv_b,
        red_x_proj,
        red_dt_proj,
        red_dt_bias,
        red_a_log,
        red_skip,
        red_out_w,
        red_state,
        red_conv_tail,
        red_seed_state,
        red_seed_rows,
    ) = (
        lax.psum_scatter(
            gain_grads.astype(jnp.bfloat16), "blk", scatter_dimension=1, tiled=True
        ).astype(jnp.float32),
        lax.psum_scatter(
            grad_w_in.astype(jnp.bfloat16), "blk", scatter_dimension=2, tiled=True
        ).astype(jnp.float32),
        lax.psum_scatter(
            grad_conv_w.astype(jnp.bfloat16), "blk", scatter_dimension=1, tiled=True
        ).astype(jnp.float32),
        lax.psum_scatter(
            grad_conv_b.astype(jnp.bfloat16), "blk", scatter_dimension=0, tiled=True
        ).astype(jnp.float32),
        lax.psum_scatter(
            grad_x_proj.astype(jnp.bfloat16), "blk", scatter_dimension=1, tiled=True
        ).astype(jnp.float32),
        lax.psum_scatter(
            grad_dt_proj.astype(jnp.bfloat16), "blk", scatter_dimension=1, tiled=True
        ).astype(jnp.float32),
        lax.psum_scatter(
            grad_dt_bias.astype(jnp.bfloat16), "blk", scatter_dimension=0, tiled=True
        ).astype(jnp.float32),
        lax.psum_scatter(
            grad_a_log.astype(jnp.bfloat16), "blk", scatter_dimension=1, tiled=True
        ).astype(jnp.float32),
        lax.psum_scatter(
            grad_skip.astype(jnp.bfloat16), "blk", scatter_dimension=0, tiled=True
        ).astype(jnp.float32),
        lax.psum_scatter(
            grad_out_w.astype(jnp.bfloat16), "blk", scatter_dimension=0, tiled=True
        ).astype(jnp.float32),
        lax.psum_scatter(
            final_state[None].astype(jnp.bfloat16), "blk", scatter_dimension=2, tiled=True
        ).astype(jnp.float32),
        lax.psum_scatter(
            tail_conv[None].astype(jnp.bfloat16), "blk", scatter_dimension=2, tiled=True
        ).astype(jnp.float32),
        lax.psum_scatter(
            grad_seed_state[None].astype(jnp.bfloat16), "blk", scatter_dimension=2, tiled=True
        ).astype(jnp.float32),
        lax.psum_scatter(
            grad_seed_rows[None].astype(jnp.bfloat16), "blk", scatter_dimension=2, tiled=True
        ).astype(jnp.float32),
    )
    summed = (
        lax.psum(red_gains.astype(jnp.bfloat16), "seqs").astype(jnp.float32),
        lax.psum(red_w_in.astype(jnp.bfloat16), "seqs").astype(jnp.float32),
        lax.psum(red_conv_w.astype(jnp.bfloat16), "seqs").astype(jnp.float32),
        lax.psum(red_conv_b.astype(jnp.bfloat16), "seqs").astype(jnp.float32),
        lax.psum(red_x_proj.astype(jnp.bfloat16), "seqs").astype(jnp.float32),
        lax.psum(red_dt_proj.astype(jnp.bfloat16), "seqs").astype(jnp.float32),
        lax.psum(red_dt_bias.astype(jnp.bfloat16), "seqs").astype(jnp.float32),
        lax.psum(red_a_log.astype(jnp.bfloat16), "seqs").astype(jnp.float32),
        lax.psum(red_skip.astype(jnp.bfloat16), "seqs").astype(jnp.float32),
        lax.psum(red_out_w.astype(jnp.bfloat16), "seqs").astype(jnp.float32),
        lax.psum(red_gate_up_one.astype(jnp.bfloat16), "seqs").astype(jnp.float32),
        lax.psum(red_down_one.astype(jnp.bfloat16), "seqs").astype(jnp.float32),
        lax.psum(red_qkv.astype(jnp.bfloat16), "seqs").astype(jnp.float32),
        lax.psum(red_wo.astype(jnp.bfloat16), "seqs").astype(jnp.float32),
        lax.psum(red_gate_up_two.astype(jnp.bfloat16), "seqs").astype(jnp.float32),
        lax.psum(red_down_two.astype(jnp.bfloat16), "seqs").astype(jnp.float32),
    )
    return (
        block_output,
        grad_now,
        red_state.astype(jnp.bfloat16),
        red_conv_tail.astype(jnp.bfloat16),
        red_tail_cache.astype(jnp.bfloat16),
        red_seed_state,
        red_seed_rows,
        red_cache_grad,
        summed[0],
        summed[1],
        summed[2],
        summed[3],
        summed[4],
        summed[5],
        summed[6],
        summed[7],
        summed[8],
        summed[9],
        summed[10],
        summed[11],
        summed[12],
        summed[13],
        summed[14],
        summed[15],
    )


def solution(mesh):
    return jax.shard_map(
        shards,
        mesh=mesh,
        in_specs=(
            P(("seqs", "blk"), None),
            P(("seqs", "blk"), None),
            P("seqs"),
            P("seqs"),
            P("seqs", None, ("blk", "mp")),
            P("seqs", None, ("blk", "mp")),
            P("seqs", None, "blk", "mp"),
            P(None, "blk"),
            P(None, None, ("blk", "mp")),
            P(None, ("blk", "mp")),
            P(("blk", "mp")),
            P(None, ("blk", "mp")),
            P(None, ("blk", "mp")),
            P(("blk", "mp")),
            P(None, ("blk", "mp")),
            P(("blk", "mp")),
            P(("blk", "mp"), None),
            P(None, None, ("blk", "mp")),
            P(("blk", "mp"), None),
            P(None, "blk", "mp"),
            P("mp", "blk"),
            P(None, None, ("blk", "mp")),
            P(("blk", "mp"), None),
        ),
        out_specs=(
            P(("seqs", "blk"), None),
            P(("seqs", "blk"), None),
            P("seqs", None, ("blk", "mp")),
            P("seqs", None, ("blk", "mp")),
            P("seqs", None, "blk", "mp"),
            P("seqs", None, ("blk", "mp")),
            P("seqs", None, ("blk", "mp")),
            P("seqs", None, "blk", "mp"),
            P(None, "blk"),
            P(None, None, ("blk", "mp")),
            P(None, ("blk", "mp")),
            P(("blk", "mp")),
            P(None, ("blk", "mp")),
            P(None, ("blk", "mp")),
            P(("blk", "mp")),
            P(None, ("blk", "mp")),
            P(("blk", "mp")),
            P(("blk", "mp"), None),
            P(None, None, ("blk", "mp")),
            P(("blk", "mp"), None),
            P(None, "blk", "mp"),
            P("mp", "blk"),
            P(None, None, ("blk", "mp")),
            P(("blk", "mp"), None),
        ),
        check_vma=False,
    )
```

profile of v0, /device:TPU:0, one launch (start us, length us, event | category | flops | bytes accessed | tf_op | source)
XLA Modules:
  0.0 3853.9 jit_solution(7321085193527237840)
XLA Ops:
  81.7 21.9 all_gather.76
  103.5 28.0 all_gather.75
  147.2 29.4 all-gather.2
  268.1 49.7 %while.87 = (s32[]{:T(128)}, bf16[3,16,512]{2,1,0:T(8,128)(2,1)}, f32[3,128,512]{1,2,0:T(8,128)}, f32[3,16,512]{2,1,0:T(8,128)S(1)}, f32[3,128,512]{2,1,0:T(8,12...) while((s32[]{:T(128)}, bf16[3,16,512]{2,1,0:T(8,128)(2,1)}, ...), condition=%wide.region_10.11_spmd, body=%wide.region_6.10_spmd.sunk | while | flops 23330816 | bytes 75907368 | solution.py:133
  353.9 219.4 %all-gather.17.cloned.1.call-done = bf16[2,1536,2048]{2,1,0:T(8,128)(2,1)} async-done(((bf16[2,1536,512]{2,1,0:T(8,128)(2,1)}), bf16[2,1536,2048]{2,1,0:T(8,128)(2,1)}) %all-gather.17.cloned.1.call-update) | async-done | bytes 12582928 | tf_op jit(solution)/shard_map/all_gather | solution.py:554
  582.7 105.5 %all-gather.19.cloned.1.call-done = bf16[2048,1536]{1,0:T(8,128)(2,1)} async-done(((bf16[512,1536]{1,0:T(8,128)(2,1)}), bf16[2048,1536]{1,0:T(8,128)(2,1)}) %all-gather.19.cloned.1.call-update) | async-done | bytes 6291472 | tf_op jit(solution)/shard_map/all_gather | solution.py:555
  696.0 107.2 %all-gather.23.cloned.1.call-done = bf16[1,2,2048,768]{3,2,1,0:T(8,128)(2,1)} async-done(((bf16[1,2,512,768]{3,2,1,0:T(8,128)(2,1)}), bf16[1,2,2048,768]{3,2,1,0:T(8,128)(2,1)}) %all-gather.23.cloned.1.call-update) | async-done | bytes 6291472 | tf_op jit(solution)/shard_map/all_gather | solution.py:543
  811.0 120.2 %all-gather.21.cloned.1.call-done = bf16[3,1536,768]{2,1,0:T(8,128)(2,1)} async-done(((bf16[3,384,768]{2,1,0:T(8,128)(2,1)}), bf16[3,1536,768]{2,1,0:T(8,128)(2,1)}) %all-gather.21.cloned.1.call-update) | async-done | bytes 7077904 | tf_op jit(solution)/shard_map/all_gather | solution.py:556
  959.7 75.4 %while.88 = (s32[]{:T(128)}, bf16[2,128,768]{2,1,0:T(8,128)(2,1)S(1)}, bf16[2,2048,768]{2,1,0:T(8,128)(2,1)}, s32[]{:T(128)}, s32[]{:T(128)}, /*index=5*/s32[]{:T(128)}, s32[]{:T(128)}, s32[]{:T(128)}, s32[]{:T(128)}) while((s32[]{:T(128)}, bf16[2,128,768]{2,1,0:T(8,128)(2,1)S(1)}, bf16[2,2048,768]{2,1,0:T(8,128)(2,1)}, s32[]{:T(128)}, ...), condition=%wide.region_16.17_spmd, body=%wide.region_15.16_spmd.sunk | while | flops 196616 | bytes 3539149 | solution.py:402
  1057.8 76.6 %all-gather.29.cloned.1.call-done = bf16[2048,1536]{1,0:T(8,128)(2,1)} async-done(((bf16[512,1536]{1,0:T(8,128)(2,1)}), bf16[2048,1536]{1,0:T(8,128)(2,1)}) %all-gather.29.cloned.1.call-update) | async-done | bytes 6291472 | tf_op jit(solution)/shard_map/all_gather | solution.py:559
  1157.9 219.4 %all-gather.27.cloned.1.call-done = bf16[2,1536,2048]{2,1,0:T(8,128)(2,1)} async-done(((bf16[2,1536,512]{2,1,0:T(8,128)(2,1)}), bf16[2,1536,2048]{2,1,0:T(8,128)(2,1)}) %all-gather.27.cloned.1.call-update) | async-done | bytes 12582928 | tf_op jit(solution)/shard_map/all_gather | solution.py:558
  1460.7 41.0 %while.89 = (s32[]{:T(128)}, f32[2,128,768]{2,1,0:T(8,128)S(1)}, s32[]{:T(128)}, f32[2,2176,768]{2,1,0:T(8,128)}, s32[]{:T(128)}, /*index=5*/s32[]{:T(128)}, s32[]{:T(128)}, s32[]{:T(128)}, s32[]{:T(128)}, s32[]{:T(128)}) while((s32[]{:T(128)}, f32[2,128,768]{2,1,0:T(8,128)S(1)}, s32[]{:T(128)}, f32[2,2176,768]{2,1,0:T(8,128)}, s32[]{:T(128)}, ...), condition=%wide.region_26.27_spmd, body=%wide.region_25.26_spmd.sunk | while | flops 786443 | bytes 4718837 | solution.py:482
  1604.4 392.6 %while.91 = (s32[]{:T(128)}, f32[128,16]{1,0:T(8,128)}, f32[128,16]{1,0:T(8,128)}, bf16[3,16,512]{2,1,0:T(8,128)(2,1)}, f32[3,128,512]{1,2,0:T(8,128)}, /*index=...) while((s32[]{:T(128)}, f32[128,16]{1,0:T(8,128)}, ...), condition=%wide.region_46.47_spmd.clone, body=%wide.region_34.46_spmd.clone.sunk | while | flops 70250496 | bytes 187967664 | solution.py:133
  2047.3 24.2 copy.292
  2161.9 136.7 %reduce-scatter.68.cloned.1.call-done = bf16[384,3072]{1,0:T(8,128)(2,1)} async-done(((bf16[1536,3072]{1,0:T(8,128)(2,1)}), bf16[384,3072]{1,0:T(8,128)(2,1)}) %reduce-scatter.68.cloned.1.call-update) | async-done | bytes 2359312
  2312.0 75.8 %reduce-scatter.46.cloned.1.call-done = bf16[384,1536]{1,0:T(8,128)(2,1)} async-done(((bf16[1536,1536]{1,0:T(8,128)(2,1)}), bf16[384,1536]{1,0:T(8,128)(2,1)}) %reduce-scatter.46.cloned.1.call-update) | async-done | bytes 1179664 | tf_op jit(solution)/shard_map/reduce_scatter | solution.py:734
  2387.8 113.6 %reduce-scatter.56.cloned.1.call-done = bf16[512,1536]{1,0:T(8,128)(2,1)} async-done(((bf16[2048,1536]{1,0:T(8,128)(2,1)}), bf16[512,1536]{1,0:T(8,128)(2,1)}) %reduce-scatter.56.cloned.1.call-update) | async-done | bytes 1572880 | tf_op jit(solution)/shard_map/reduce_scatter | solution.py:640
  2501.4 114.2 %reduce-scatter.50.cloned.1.call-done = bf16[512,1536]{1,0:T(8,128)(2,1)} async-done(((bf16[2048,1536]{1,0:T(8,128)(2,1)}), bf16[512,1536]{1,0:T(8,128)(2,1)}) %reduce-scatter.50.cloned.1.call-update) | async-done | bytes 1572880 | tf_op jit(solution)/shard_map/reduce_scatter | solution.py:668
  2615.6 126.2 %reduce-scatter.52.cloned.1.call-done = bf16[3,384,768]{2,1,0:T(8,128)(2,1)} async-done(((bf16[3,1536,768]{2,1,0:T(8,128)(2,1)}), bf16[3,384,768]{2,1,0:T(8,128)(2,1)}) %reduce-scatter.52.cloned.1.call-update) | async-done | bytes 1769488 | tf_op jit(solution)/shard_map/reduce_scatter | solution.py:648
  2741.8 214.8 %reduce-scatter.54.cloned.1.call-done = bf16[2,1536,512]{2,1,0:T(8,128)(2,1)} async-done(((bf16[2,1536,2048]{2,1,0:T(8,128)(2,1)}), bf16[2,1536,512]{2,1,0:T(8,128)(2,1)}) %reduce-scatter.54.cloned.1.call-update) | async-done | bytes 3145744 | tf_op jit(solution)/shard_map/reduce_scatter | solution.py:637
  2956.6 215.2 %reduce-scatter.48.cloned.1.call-done = bf16[2,1536,512]{2,1,0:T(8,128)(2,1)} async-done(((bf16[2,1536,2048]{2,1,0:T(8,128)(2,1)}), bf16[2,1536,512]{2,1,0:T(8,128)(2,1)}) %reduce-scatter.48.cloned.1.call-update) | async-done | bytes 3145744 | tf_op jit(solution)/shard_map/reduce_scatter | solution.py:665
  3346.9 90.9 %reduce-scatter.44.cloned.1.call-done = bf16[1,2,512,768]{3,2,1,0:T(8,128)(2,1)} async-done(((bf16[1,2,2048,768]{3,2,1,0:T(8,128)(2,1)}), bf16[1,2,512,768]{3,2,1,0:T(8,128)(2,1)}) %reduce-scatter.44.cloned.1.call-update) | async-done | bytes 1572880 | tf_op jit(solution)/shard_map/reduce_scatter | solution.py:657
  3441.1 291.6 %all-reduce.105.cloned.1.call-done = (bf16[2,1536,384]{2,1,0:T(8,128)(2,1)}, bf16[128,384]{1,0:T(8,128)(2,1)}, bf16[96,384]{1,0:T(8,128)(2,1)}, bf16[384,1536]{1...) async-done(((bf16[2,1536,384]{2,1,0:T(8,128)(2,1)}, ...) | async-done | bytes 15507472 | tf_op jit(solution)/shard_map/psum | solution.py:752
  3755.3 91.9 %reduce-scatter.42.cloned.1.call-done = bf16[1,2,512,768]{3,2,1,0:T(8,128)(2,1)} async-done(((bf16[1,2,2048,768]{3,2,1,0:T(8,128)(2,1)}), bf16[1,2,512,768]{3,2,1,0:T(8,128)(2,1)}) %reduce-scatter.42.cloned.1.call-update) | async-done | bytes 1572880 | tf_op jit(solution)/shard_map/reduce_scatter | solution.py:654
  (1622 shorter events, 1446.3 us)
Async XLA Ops:
  329.3 359.0 %all-gather.19.cloned.1.call-start = ((), (), s32[]{:S(2)}) async-start(), calls=%async_computation.23 | async-start | bytes 7864320 | tf_op jit(solution)/shard_map/all_gather | solution.py:555
  329.9 473.3 %all-gather.23.cloned.1.call-start = ((), (), s32[]{:S(2)}) async-start(), calls=%async_computation.26 | async-start | bytes 7864320 | tf_op jit(solution)/shard_map/all_gather | solution.py:543
  330.5 600.7 %all-gather.21.cloned.1.call-start = ((), (), s32[]{:S(2)}) async-start(), calls=%async_computation.25 | async-start | bytes 8847360 | tf_op jit(solution)/shard_map/all_gather | solution.py:556
  331.2 619.5 %all-reduce.95.cloned.1.call-start = ((), (), s32[]{:S(2)}) async-start(), calls=%async_computation.24 | async-start | bytes 786432 | tf_op jit(solution)/shard_map/psum | solution.py:37
  692.8 360.8 %all-gather.25.cloned.1.call-start = ((), (), s32[]{:S(2)}) async-start(), calls=%async_computation.27 | async-start | bytes 2949120 | tf_op jit(solution)/shard_map/all_gather | solution.py:557
  693.5 440.8 %all-gather.29.cloned.1.call-start = ((), (), s32[]{:S(2)}) async-start(), calls=%async_computation.30 | async-start | bytes 7864320 | tf_op jit(solution)/shard_map/all_gather | solution.py:559
  694.1 462.3 %all-reduce.97.cloned.1.call-start = ((), (), s32[]{:S(2)}) async-start(), calls=%async_computation.28 | async-start | bytes 786432 | tf_op jit(solution)/shard_map/psum | solution.py:37
  1057.3 353.0 %all-reduce.99.cloned.1.call-start = ((), (), s32[]{:S(2)}) async-start(), calls=%async_computation.31 | async-start | bytes 786432 | tf_op jit(solution)/shard_map/psum | solution.py:37
  1548.9 599.0 %all-reduce.107.cloned.1.call-start = ((), (), s32[]{:S(2)}) async-start(), calls=%async_computation.54 | async-start | bytes 1572864 | tf_op jit(solution)/shard_map/psum | solution.py:37
  2086.1 415.4 %reduce-scatter.56.cloned.1.call-start = ((), (), s32[]{:S(2)}) async-start(), calls=%async_computation.41 | async-start | bytes 7864320 | tf_op jit(solution)/shard_map/reduce_scatter | solution.py:640
  2091.9 523.7 %reduce-scatter.50.cloned.1.call-start = ((), (), s32[]{:S(2)}) async-start(), calls=%async_computation.38 | async-start | bytes 7864320 | tf_op jit(solution)/shard_map/reduce_scatter | solution.py:668
  2097.8 644.1 %reduce-scatter.52.cloned.1.call-start = ((), (), s32[]{:S(2)}) async-start(), calls=%async_computation.39 | async-start | bytes 8847360 | tf_op jit(solution)/shard_map/reduce_scatter | solution.py:648
  2104.8 851.8 %reduce-scatter.54.cloned.1.call-start = ((), (), s32[]{:S(2)}) async-start(), calls=%async_computation.40 | async-start | bytes 15728640 | tf_op jit(solution)/shard_map/reduce_scatter | solution.py:637
  2115.1 1056.7 %reduce-scatter.48.cloned.1.call-start = ((), (), s32[]{:S(2)}) async-start(), calls=%async_computation.37 | async-start | bytes 15728640 | tf_op jit(solution)/shard_map/reduce_scatter | solution.py:665
  2125.3 1071.1 %reduce-scatter.60.cloned.1.call-start = ((), (), s32[]{:S(2)}) async-start(), calls=%async_computation.43 | async-start | bytes 491520
  2127.4 1090.8 %reduce-scatter.58.cloned.1.call-start = ((), (), s32[]{:S(2)}) async-start(), calls=%async_computation.42 | async-start | bytes 491520
  2129.0 1111.0 %reduce-scatter.64.cloned.1.call-start = ((), (), s32[]{:S(2)}) async-start(), calls=%async_computation.45 | async-start | bytes 491520
  2144.1 1117.4 %reduce-scatter.70.cloned.1.call-start = ((), (), s32[]{:S(2)}) async-start(), calls=%async_computation.48 | async-start | bytes 491520
  2145.2 1138.2 %reduce-scatter.62.cloned.1.call-start = ((), (), s32[]{:S(2)}) async-start(), calls=%async_computation.44 | async-start | bytes 491520
  2146.8 1157.9 %reduce-scatter.76.cloned.1.call-start = ((), (), s32[]{:S(2)}) async-start(), calls=%async_computation.51 | async-start | bytes 491520
  2147.9 1178.0 %reduce-scatter.66.cloned.1.call-start = ((), (), s32[]{:S(2)}) async-start(), calls=%async_computation.46 | async-start | bytes 491520
  2150.3 1287.5 %reduce-scatter.44.cloned.1.call-start = ((), (), s32[]{:S(2)}) async-start(), calls=%async_computation.35 | async-start | bytes 7864320 | tf_op jit(solution)/shard_map/reduce_scatter | solution.py:657
  2156.3 1576.4 %all-reduce.105.cloned.1.call-start = ((), (), s32[]{:S(2)}) async-start(), calls=%async_computation.53 | async-start | bytes 31014912 | tf_op jit(solution)/shard_map/psum | solution.py:752
  3171.8 675.4 %reduce-scatter.42.cloned.1.call-start = ((), (), s32[]{:S(2)}) async-start(), calls=%async_computation.34 | async-start | bytes 7864320 | tf_op jit(solution)/shard_map/reduce_scatter | solution.py:654
  (390 other events, 10895.3 us)
Sparse Core Ops, SparseCore 0:
  9.6 181.6 all-gather.12
  192.9 88.2 all-gather.14
  328.8 23.5 all-reduce.92
  353.9 219.3 all-gather.16
  574.7 113.5 all-gather.18
  689.7 113.4 all-gather.22
  804.8 126.3 all-gather.20
  952.3 64.5 all-gather.24
  1018.4 115.9 all-gather.28
  1157.9 219.3 all-gather.26
  1549.0 19.6 all-reduce.102
  2043.2 21.9 reduce-scatter.73
  2089.8 45.9 reduce-scatter.77
  2138.0 160.5 reduce-scatter.67
  2301.5 86.2 reduce-scatter.45
  2390.1 111.2 reduce-scatter.55
  2504.3 111.2 reduce-scatter.49
  2617.8 124.0 reduce-scatter.51
  2744.2 212.3 reduce-scatter.53
  2958.8 212.8 reduce-scatter.47
  3174.5 21.8 reduce-scatter.59
  3328.7 109.0 reduce-scatter.43
  3444.4 288.2 all-reduce.104
  3735.4 111.7 reduce-scatter.41
  (12 shorter events, 222.6 us)
where the time goes:
time: 3880 us; the launch traced here: 3850 us
  waiting for transfers between devices  2650 us (68%)
  local copies, waits for them, and re-layouts  456 us (12%)
  other arithmetic  292 us (8%)
  blocking collectives  232 us (6%)
  matrix products  153 us (4%)
  starting transfers between devices  48.3 us (1%)
    psum x1, waiting for transfers between devices, shards(): lax.psum(red_w_in.astype(jnp.bfloat16), 'seqs').astype(jnp.float32)  292 us
    unnamed x47, waiting for transfers between devices  250 us
    all_gather x1, waiting for transfers between devices, shards(): lax.all_gather(ffn2_gate_up, 'blk', axis=2, tiled=True)  219 us
    all_gather x1, waiting for transfers between devices, shards(): lax.all_gather(ffn1_gate_up, 'blk', axis=2, tiled=True)  219 us
    reduce_scatter x1, waiting for transfers between devices, shards(): lax.psum_scatter(grad_gate_up_one.astype(jnp.bfloat16), 'blk', scatter_di...  215 us
    reduce_scatter x1, waiting for transfers between devices, shards(): lax.psum_scatter(grad_gate_up_two.astype(jnp.bfloat16), 'blk', scatter_di...  215 us
    pad x114, local copies, waits for them, and re-layouts, scan_piece(): lax.associative_scan(pair_combine, (shrink[:, -1], inner_state[:, -1]))  155 us
    reduce_scatter x1, waiting for transfers between devices, shards(): lax.psum_scatter(grad_qkv.astype(jnp.bfloat16), 'blk', scatter_dimension=...  126 us
  transfers between devices with their start and end apart: 50, of which 43 were waited for; matrix products, arithmetic and copies ran while one was open for 9% of the time, Pallas kernels for 0%

commit v1 on v0

v1 whole, which is shorter than its diff:
```python
import jax
import jax.numpy as jnp
from jax import lax
from jax.experimental import pallas as pl
from jax.experimental.pallas import tpu as pltpu
from jax.sharding import PartitionSpec as P

HD = 128
EPSILON = 1e-05
ROPE_BASE = 10000.0
NEG_BIG = -1e30
DIRECT_MAX = 4
BF = jnp.bfloat16
F32 = jnp.float32


def matmul(left_op, right_op):
    return jnp.dot(left_op, right_op, preferred_element_type=F32)


def matmul_tn(left_op, right_op):
    return lax.dot_general(left_op, right_op, (((0,), (0,)), ((), ())), preferred_element_type=F32)


def matmul_nt(left_op, right_op):
    return lax.dot_general(left_op, right_op, (((1,), (1,)), ((), ())), preferred_element_type=F32)


def direct():
    return lax.axis_size("blk") <= DIRECT_MAX


def from_ahead(value, steps):
    count = lax.axis_size("blk")
    return lax.ppermute(value, "blk", [((i + steps) % count, i) for i in range(count)])


def to_ahead(value, steps):
    count = lax.axis_size("blk")
    return lax.ppermute(value, "blk", [(i, (i + steps) % count) for i in range(count)])


def mp_swap(value):
    return lax.ppermute(value, "mp", [(0, 1), (1, 0)])


def by_order(first, own, other):
    return jnp.stack([jnp.where(first, own, other), jnp.where(first, other, own)])


def blk_ordered(pieces):
    count = len(pieces)
    dev_index = lax.axis_index("blk")
    ordered = []
    for place in range(count):
        distance = (place - dev_index) % count
        chosen = pieces[0]
        for steps in range(1, count):
            chosen = jnp.where(distance == steps, pieces[steps], chosen)
        ordered.append(chosen)
    return ordered


def gather_rows(rows, ordered):
    if not direct():
        return lax.all_gather(rows, ("blk", "mp"), axis=0, tiled=True)
    count = lax.axis_size("blk")
    pieces = [rows] + [from_ahead(rows, steps) for steps in range(1, count)]
    others = [mp_swap(piece) for piece in pieces]
    if not ordered:
        return jnp.concatenate(pieces + others, axis=0)
    first = lax.axis_index("mp") == 0
    own_in, other_in = (blk_ordered(pieces), blk_ordered(others))
    laid = []
    for own, other in zip(own_in, other_in):
        laid += [jnp.where(first, own, other), jnp.where(first, other, own)]
    return jnp.concatenate(laid, axis=0)


def scatter_rows(partial, ordered):
    if not direct():
        return lax.psum_scatter(
            partial.astype(BF), ("blk", "mp"), scatter_dimension=0, tiled=True
        ).astype(F32)
    count = lax.axis_size("blk")
    rows = partial.shape[0] // (2 * count)
    width = partial.shape[1]
    dev_index = lax.axis_index("blk")
    part = lax.axis_index("mp")
    if ordered:
        split = partial.astype(BF).reshape(count, 2, rows, width)
        mine = lax.dynamic_index_in_dim(split, part, 1, keepdims=False)
        theirs = lax.dynamic_index_in_dim(split, 1 - part, 1, keepdims=False)
    else:
        split = partial.astype(BF).reshape(2, count, rows, width)
        mine, theirs = (split[0], split[1])
    both = (mine.astype(F32) + mp_swap(theirs).astype(F32)).astype(BF)
    total = None
    for steps in range(count - 1, -1, -1):
        if ordered:
            chunk = lax.dynamic_index_in_dim(both, (dev_index + steps) % count, 0, keepdims=False)
        else:
            chunk = both[steps]
        arrived = (to_ahead(chunk, steps) if steps else chunk).astype(F32)
        total = arrived if total is None else total + arrived
    return total


def sum_small(partial):
    if not direct():
        return lax.psum(partial.astype(BF), ("blk", "mp")).astype(F32)
    count = lax.axis_size("blk")
    part = lax.axis_index("mp")
    split = partial.reshape(2, partial.shape[0] // 2, partial.shape[1])
    mine = lax.dynamic_index_in_dim(split, part, 0, keepdims=False)
    theirs = lax.dynamic_index_in_dim(split, 1 - part, 0, keepdims=False)
    both = (mine + mp_swap(theirs)).astype(BF)
    total = both.astype(F32)
    for steps in range(1, count):
        total = total + from_ahead(both, steps).astype(F32)
    return by_order(part == 0, total, mp_swap(total)).reshape(partial.shape)


def blk_all(value):
    if not direct():
        return lax.all_gather(value, "blk", axis=0)
    return jnp.stack([value] + [from_ahead(value, s) for s in range(1, lax.axis_size("blk"))])


def blk_gather_cols(value):
    if not direct():
        return lax.all_gather(value, "blk", axis=1, tiled=True)
    pieces = [value] + [from_ahead(value, s) for s in range(1, lax.axis_size("blk"))]
    return jnp.concatenate(blk_ordered(pieces), axis=1)


def blk_gather_rows(value):
    if not direct():
        return lax.all_gather(value, "blk", axis=0, tiled=True)
    pieces = [value] + [from_ahead(value, s) for s in range(1, lax.axis_size("blk"))]
    return jnp.concatenate(blk_ordered(pieces), axis=0)


def blk_scatter(partial, axis):
    count = lax.axis_size("blk")
    if not direct():
        return lax.psum_scatter(partial, "blk", scatter_dimension=axis, tiled=True).astype(F32)
    size = partial.shape[axis] // count
    dev_index = lax.axis_index("blk")
    total = None
    for steps in range(count - 1, -1, -1):
        chunk = lax.dynamic_slice_in_dim(partial, ((dev_index + steps) % count) * size, size, axis)
        arrived = (to_ahead(chunk, steps) if steps else chunk).astype(F32)
        total = arrived if total is None else total + arrived
    return total


def seq_sum(value):
    low = value.astype(BF)
    rows = low.shape[0]
    if lax.axis_size("seqs") != 4 or rows % 8:
        return lax.psum(low, "seqs").astype(F32)
    index = lax.axis_index("seqs")
    bits = (index % 2, index // 2)
    pairs = ([(0, 1), (1, 0), (2, 3), (3, 2)], [(0, 2), (2, 0), (1, 3), (3, 1)])

    def exchange(array, way):
        return lax.ppermute(array, "seqs", pairs[way])

    def halve(array, way):
        split = array.reshape(2, array.shape[0] // 2, array.shape[1])
        keep = lax.dynamic_index_in_dim(split, bits[way], 0, keepdims=False)
        send = lax.dynamic_index_in_dim(split, 1 - bits[way], 0, keepdims=False)
        return (keep.astype(F32) + exchange(send, way).astype(F32)).astype(BF)

    def double(array, way):
        pair = by_order(bits[way] == 0, array, exchange(array, way))
        return pair.reshape(2 * array.shape[0], array.shape[1])

    halves = []
    for begin, first, second in ((0, 0, 1), (rows // 2, 1, 0)):
        piece = low[begin : begin + rows // 2]
        piece = halve(halve(piece, first), second)
        halves.append(double(double(piece, second), first))
    return jnp.concatenate(halves, axis=0).astype(F32)


def norm_forward(values, norm_gain):
    inverse = lax.rsqrt(jnp.mean(values * values, axis=-1, keepdims=True) + EPSILON)
    unit_rows = values * inverse
    return ((unit_rows * norm_gain).astype(BF), unit_rows, inverse)


def norm_backward(grad_out, unit_rows, inverse, norm_gain):
    grad_unit = grad_out * norm_gain
    grad_gain = jnp.sum(grad_out * unit_rows, axis=0)
    grad_in = inverse * (
        grad_unit - unit_rows * jnp.mean(grad_unit * unit_rows, axis=-1, keepdims=True)
    )
    return (grad_in, grad_gain)


def silu_slope(values):
    logistic = jax.nn.sigmoid(values)
    return logistic * (1.0 + values * (1.0 - logistic))


def rotation_tables(positions):
    half_dim = HD // 2
    frequency = ROPE_BASE ** (-(jnp.arange(half_dim, dtype=F32) * 2.0 / HD))
    angles = positions.astype(F32)[:, None] * frequency[None, :]
    return (jnp.cos(angles), jnp.sin(angles))


def rotate(values, cosine, sine_part, direction):
    count_rows = values.shape[0]
    by_head = values.reshape(count_rows, -1, HD)
    half_dim = HD // 2
    cos_rows = cosine[:, None, :]
    sin_rows = direction * sine_part[:, None, :]
    first_half = by_head[..., :half_dim]
    second_half = by_head[..., half_dim:]
    turned = jnp.concatenate(
        [
            first_half * cos_rows - second_half * sin_rows,
            second_half * cos_rows + first_half * sin_rows,
        ],
        axis=-1,
    )
    return turned.reshape(count_rows, -1)


def wide(array, times):
    return array if times == 1 else jnp.concatenate([array] * times, axis=1)


def scan_fwd_kernel(
    step_ref, u_ref, in_ref, out_ref, dec_ref, h0_ref, y_ref, hp_ref, hf_ref, h_scr
):
    @pl.when(pl.program_id(0) == 0)
    def _():
        h_scr[...] = h0_ref[...]

    decay = dec_ref[...]
    times = decay.shape[1] // in_ref.shape[2]

    def group(turn, state):
        base = pl.multiple_of(turn * 8, 8)
        steps = step_ref[pl.ds(base, 8), :]
        drives = u_ref[pl.ds(base, 8), :]
        outs = []
        for j in range(8):
            hp_ref[base + j] = state
            shrink = jnp.exp(steps[j : j + 1, :] * decay)
            state = shrink * state + wide(in_ref[base + j], times) * drives[j : j + 1, :]
            outs.append(jnp.sum(wide(out_ref[base + j], times) * state, axis=0, keepdims=True))
        y_ref[pl.ds(base, 8), :] = jnp.concatenate(outs, axis=0)
        return state

    state = lax.fori_loop(0, step_ref.shape[0] // 8, group, h_scr[...])
    h_scr[...] = state
    hf_ref[...] = state


def scan_bwd_kernel(
    step_ref,
    u_ref,
    gy_ref,
    in_ref,
    out_ref,
    hp_ref,
    dec_ref,
    gu_ref,
    gs_ref,
    gin_ref,
    gout_ref,
    gdec_ref,
    gh_ref,
    a_scr,
    d_scr,
):
    @pl.when(pl.program_id(0) == 0)
    def _():
        a_scr[...] = jnp.zeros_like(a_scr)
        d_scr[...] = jnp.zeros_like(d_scr)

    decay = dec_ref[...]
    lanes = in_ref.shape[2]
    times = decay.shape[1] // lanes
    groups = step_ref.shape[0] // 8

    def fold(array):
        total = array[:, :lanes]
        for k in range(1, times):
            total = total + array[:, k * lanes : (k + 1) * lanes]
        return total

    def group(turn, carried):
        adj, grad_decay = carried
        base = pl.multiple_of((groups - 1 - turn) * 8, 8)
        steps = step_ref[pl.ds(base, 8), :]
        drives = u_ref[pl.ds(base, 8), :]
        grads = gy_ref[pl.ds(base, 8), :]
        gus, gss = ([], [])
        for j in range(7, -1, -1):
            step_row, u_row, gy_row = (
                steps[j : j + 1, :],
                drives[j : j + 1, :],
                grads[j : j + 1, :],
            )
            in_now = wide(in_ref[base + j], times)
            before = hp_ref[base + j]
            shrink = jnp.exp(step_row * decay)
            kept = shrink * before
            state = kept + in_now * u_row
            adj = adj + wide(out_ref[base + j], times) * gy_row
            gout_ref[base + j] = fold(state * gy_row)
            gin_ref[base + j] = fold(adj * u_row)
            gus.append(jnp.sum(adj * in_now, axis=0, keepdims=True))
            grad_exp = adj * kept
            gss.append(jnp.sum(grad_exp * decay, axis=0, keepdims=True))
            grad_decay = grad_decay + grad_exp * step_row
            adj = shrink * adj
        gu_ref[pl.ds(base, 8), :] = jnp.concatenate(gus[::-1], axis=0)
        gs_ref[pl.ds(base, 8), :] = jnp.concatenate(gss[::-1], axis=0)
        return (adj, grad_decay)

    adj, grad_decay = lax.fori_loop(0, groups, group, (a_scr[...], d_scr[...]))
    a_scr[...] = adj
    d_scr[...] = grad_decay
    gh_ref[...] = adj
    gdec_ref[...] = grad_decay


def scan_forward(entering, step, drive, in_b, out_b, decay):
    rows, chans = step.shape
    states, lanes = (decay.shape[0], in_b.shape[2])
    block = min(128, rows)
    row_spec = pl.BlockSpec((block, chans), lambda i: (i, 0))
    coef_spec = pl.BlockSpec((block, states, lanes), lambda i: (i, 0, 0))
    hist_spec = pl.BlockSpec((block, states, chans), lambda i: (i, 0, 0))
    fixed = pl.BlockSpec((states, chans), lambda i: (0, 0))
    return pl.pallas_call(
        scan_fwd_kernel,
        grid=(rows // block,),
        in_specs=[row_spec, row_spec, coef_spec, coef_spec, fixed, fixed],
        out_specs=[row_spec, hist_spec, fixed],
        out_shape=[
            jax.ShapeDtypeStruct((rows, chans), F32),
            jax.ShapeDtypeStruct((rows, states, chans), F32),
            jax.ShapeDtypeStruct((states, chans), F32),
        ],
        scratch_shapes=[pltpu.VMEM((states, chans), F32)],
        name="scan_fwd",
    )(step, drive, in_b, out_b, decay, entering)


def scan_backward(step, drive, grad_y, in_b, out_b, before, decay):
    rows, chans = step.shape
    states, lanes = (decay.shape[0], in_b.shape[2])
    block = min(128, rows)
    last = rows // block - 1
    row_spec = pl.BlockSpec((block, chans), lambda i: (last - i, 0))
    coef_spec = pl.BlockSpec((block, states, lanes), lambda i: (last - i, 0, 0))
    hist_spec = pl.BlockSpec((block, states, chans), lambda i: (last - i, 0, 0))
    fixed = pl.BlockSpec((states, chans), lambda i: (0, 0))
    return pl.pallas_call(
        scan_bwd_kernel,
        grid=(rows // block,),
        in_specs=[row_spec, row_spec, row_spec, coef_spec, coef_spec, hist_spec, fixed],
        out_specs=[row_spec, row_spec, coef_spec, coef_spec, fixed, fixed],
        out_shape=[
            jax.ShapeDtypeStruct((rows, chans), F32),
            jax.ShapeDtypeStruct((rows, chans), F32),
            jax.ShapeDtypeStruct((rows, states, lanes), F32),
            jax.ShapeDtypeStruct((rows, states, lanes), F32),
            jax.ShapeDtypeStruct((states, chans), F32),
            jax.ShapeDtypeStruct((states, chans), F32),
        ],
        scratch_shapes=[pltpu.VMEM((states, chans), F32), pltpu.VMEM((states, chans), F32)],
        name="scan_bwd",
    )(step, drive, grad_y, in_b, out_b, before, decay)


def masked_scores(queries, keys, allowed):
    scores = lax.dot_general(
        queries, keys, (((1,), (1,)), ((), ())), preferred_element_type=F32
    ) * HD ** (-0.5)
    return jnp.where(allowed, scores, NEG_BIG)


def allowed_keys(qpos_ref, kpos_ref, window):
    query_at, key_at = (qpos_ref[...], kpos_ref[...])
    return (key_at > query_at - window) & (key_at <= query_at)


def attend_fwd_kernel(window, q_ref, k_ref, v_ref, qpos_ref, kpos_ref, o_ref, stat_ref):
    allowed = allowed_keys(qpos_ref, kpos_ref, window)
    lane = lax.broadcasted_iota(jnp.int32, stat_ref.shape, 1)
    stats = jnp.zeros(stat_ref.shape, F32)
    for head in range(q_ref.shape[1] // HD):
        cols = slice(head * HD, (head + 1) * HD)
        scores = masked_scores(q_ref[:, cols], k_ref[:, cols], allowed)
        row_max = jnp.max(scores, axis=1, keepdims=True)
        weights = jnp.exp(scores - row_max)
        row_sum = jnp.sum(weights, axis=1, keepdims=True)
        o_ref[:, cols] = jnp.dot(weights.astype(BF), v_ref[:, cols], preferred_element_type=F32)
        stats = jnp.where(lane == head, row_max, stats)
        stats = jnp.where(lane == head + HD // 2, row_sum, stats)
    stat_ref[...] = stats


def attend_bwd_kernel(
    window, q_ref, k_ref, v_ref, go_ref, stat_ref, qpos_ref, kpos_ref, gq_ref, gk_ref, gv_ref
):
    @pl.when(pl.program_id(0) == 0)
    def _():
        gk_ref[...] = jnp.zeros_like(gk_ref)
        gv_ref[...] = jnp.zeros_like(gv_ref)

    allowed = allowed_keys(qpos_ref, kpos_ref, window)
    scale = HD ** (-0.5)
    for head in range(q_ref.shape[1] // HD):
        cols = slice(head * HD, (head + 1) * HD)
        queries, keys, grads = (q_ref[:, cols], k_ref[:, cols], go_ref[:, cols])
        scores = masked_scores(queries, keys, allowed)
        probs = jnp.exp(scores - stat_ref[:, head : head + 1])
        grad_prob = lax.dot_general(
            grads, v_ref[:, cols], (((1,), (1,)), ((), ())), preferred_element_type=F32
        )
        delta = stat_ref[:, head + HD // 2 : head + HD // 2 + 1]
        grad_scores = (probs * (grad_prob - delta)).astype(BF)
        gq_ref[:, cols] = jnp.dot(grad_scores, keys, preferred_element_type=F32) * scale
        gk_ref[:, cols] += matmul_tn(grad_scores, queries) * scale
        gv_ref[:, cols] += matmul_tn(probs.astype(BF), grads)


def attend_forward(queries, keys, values, query_pos, key_pos, window):
    rows, width = queries.shape
    count = keys.shape[0]
    block = min(256, rows)
    row_spec = pl.BlockSpec((block, width), lambda i: (i, 0))
    key_spec = pl.BlockSpec((count, width), lambda i: (0, 0))
    return pl.pallas_call(
        lambda *refs: attend_fwd_kernel(window, *refs),
        grid=(rows // block,),
        in_specs=[
            row_spec,
            key_spec,
            key_spec,
            pl.BlockSpec((block, 1), lambda i: (i, 0)),
            pl.BlockSpec((1, count), lambda i: (0, 0)),
        ],
        out_specs=[row_spec, pl.BlockSpec((block, HD), lambda i: (i, 0))],
        out_shape=[
            jax.ShapeDtypeStruct((rows, width), F32),
            jax.ShapeDtypeStruct((rows, HD), F32),
        ],
        name="attend_fwd",
    )(queries, keys, values, query_pos, key_pos)


def attend_backward(queries, keys, values, grads, stats, query_pos, key_pos, window):
    rows, width = queries.shape
    count = keys.shape[0]
    block = min(256, rows)
    row_spec = pl.BlockSpec((block, width), lambda i: (i, 0))
    key_spec = pl.BlockSpec((count, width), lambda i: (0, 0))
    return pl.pallas_call(
        lambda *refs: attend_bwd_kernel(window, *refs),
        grid=(rows // block,),
        in_specs=[
            row_spec,
            key_spec,
            key_spec,
            row_spec,
            pl.BlockSpec((block, HD), lambda i: (i, 0)),
            pl.BlockSpec((block, 1), lambda i: (i, 0)),
            pl.BlockSpec((1, count), lambda i: (0, 0)),
        ],
        out_specs=[row_spec, key_spec, key_spec],
        out_shape=[
            jax.ShapeDtypeStruct((rows, width), F32),
            jax.ShapeDtypeStruct((count, width), F32),
            jax.ShapeDtypeStruct((count, width), F32),
        ],
        name="attend_bwd",
    )(queries, keys, values, grads, stats, query_pos, key_pos)


def ffn_forward(rows, gain, gate_up, down, valid):
    normed, unit, inverse = norm_forward(rows, gain)
    full = gather_rows(normed, False)
    gate, up = (matmul(full, gate_up[0]), matmul(full, gate_up[1]))
    hidden = (jax.nn.silu(gate) * up).astype(BF)
    after = rows + valid * scatter_rows(matmul(hidden, down), False)
    return (after, (full, unit, inverse, gate, up, hidden))


def ffn_backward(grad_after, kept, gain, gate_up, down, valid):
    full, unit, inverse, gate, up, hidden = kept
    branch = gather_rows((valid * grad_after).astype(BF), False)
    grad_hidden = matmul_nt(branch, down)
    grad_gate = (grad_hidden * up * silu_slope(gate)).astype(BF)
    grad_up = (grad_hidden * jax.nn.silu(gate)).astype(BF)
    grad_normed = scatter_rows(
        matmul_nt(grad_gate, gate_up[0]) + matmul_nt(grad_up, gate_up[1]), False
    )
    grad_in, grad_gain = norm_backward(grad_normed, unit, inverse, gain)
    grad_down = matmul_tn(hidden, branch)
    grad_gate_up = jnp.concatenate([matmul_tn(full, grad_gate), matmul_tn(full, grad_up)], axis=0)
    return (grad_after + grad_in, grad_gain, grad_gate_up, grad_down)


def shards(
    block_input,
    cotangent,
    lengths,
    offsets,
    ssm_state,
    conv_state,
    kv_cache,
    norm_gains,
    w_in,
    conv_weight,
    conv_bias,
    x_proj,
    dt_proj,
    dt_bias,
    a_log,
    d_skip,
    mamba_out,
    ffn1_gate_up,
    ffn1_down,
    qkv_proj,
    attn_out,
    ffn2_gate_up,
    ffn2_down,
):
    blocks = lax.axis_size("blk")
    dev_index = lax.axis_index("blk")
    part = lax.axis_index("mp")
    first = part == 0
    tok_rows, model = block_input.shape
    own_rows = tok_rows // 2
    total_rows = tok_rows * blocks
    seq_len = lengths[0]
    offset = offsets[0]
    window = kv_cache.shape[2] * blocks
    cache_rows = kv_cache.shape[2]

    qkv_full = lax.all_gather(qkv_proj, "blk", axis=1, tiled=True)
    out_full = lax.all_gather(attn_out, "blk", axis=1, tiled=True)

    gains = blk_gather_cols(norm_gains).astype(F32)
    rows_in = lax.dynamic_slice_in_dim(block_input, part * own_rows, own_rows, 0)
    grad_rows = lax.dynamic_slice_in_dim(cotangent, part * own_rows, own_rows, 0)
    own_pos = dev_index * tok_rows + part * own_rows + jnp.arange(own_rows, dtype=jnp.int32)
    valid = (own_pos < seq_len).astype(F32)[:, None]
    token_at = jnp.arange(total_rows, dtype=jnp.int32)
    valid_all = (token_at < seq_len).astype(F32)[:, None]

    normed_m, unit_m, inverse_m = norm_forward(rows_in, gains[0])
    full_m = gather_rows(normed_m, True)
    x_low = matmul(full_m, w_in[0]).astype(BF)
    z_lin = matmul(full_m, w_in[1])
    taps = conv_weight.shape[0]
    conv_w = conv_weight.astype(F32)
    padded = jnp.concatenate([conv_state[0], x_low], axis=0)
    padded_f = padded.astype(F32)
    conv_pre = conv_bias.astype(F32) + sum(
        (conv_w[k] * padded_f[k : k + total_rows] for k in range(taps))
    )
    conv_out = jax.nn.silu(conv_pre)
    conv_low = conv_out.astype(BF)
    rank = dt_proj.shape[0]
    states, chans = a_log.shape
    projected = sum_small(matmul_nt(conv_low, x_proj))
    dt_low = projected[:, :rank].astype(BF)
    lanes = min(chans, 128)
    spread = (total_rows, states, lanes)
    in_b = jnp.broadcast_to(projected[:, rank : rank + states, None], spread)
    out_b = jnp.broadcast_to(projected[:, rank + states :, None], spread)
    dt_lin = matmul(dt_low, dt_proj) + dt_bias.astype(F32)
    step = jax.nn.softplus(dt_lin) * valid_all
    decay = -jnp.exp(a_log.astype(F32))
    drive = step * conv_out
    scanned, before, final_state = scan_forward(
        ssm_state[0].astype(F32), step, drive, in_b, out_b, decay
    )
    skip = d_skip.astype(F32)
    mixed = scanned + skip * conv_out
    gated = (mixed * jax.nn.silu(z_lin)).astype(BF)
    rows_m = rows_in + valid * scatter_rows(matmul(gated, mamba_out), True)
    new_conv = lax.dynamic_slice_in_dim(padded, seq_len, taps - 1, 0)

    rows_one, kept_one = ffn_forward(rows_m, gains[1], ffn1_gate_up, ffn1_down, valid)

    normed_a, unit_a, inverse_a = norm_forward(rows_one, gains[2])
    full_a = gather_rows(normed_a, True)
    cosine, sine = rotation_tables(offset + token_at)
    q_low = rotate(matmul(full_a, qkv_full[0]), cosine, sine, 1.0).astype(BF)
    k_low = rotate(matmul(full_a, qkv_full[1]), cosine, sine, 1.0).astype(BF)
    v_low = matmul(full_a, qkv_full[2]).astype(BF)
    width = q_low.shape[1]
    heads = width // HD
    first_pos = dev_index * tok_rows

    def own_block(array):
        return lax.dynamic_slice_in_dim(array, first_pos, tok_rows, 0)

    keys = jnp.concatenate([kv_cache[0, 0], own_block(k_low)], axis=0)
    values = jnp.concatenate([kv_cache[0, 1], own_block(v_low)], axis=0)
    cache_at = dev_index * cache_rows - window + jnp.arange(cache_rows, dtype=jnp.int32)
    fresh_at = first_pos + jnp.arange(tok_rows, dtype=jnp.int32)
    fresh_at = jnp.where(fresh_at < seq_len, fresh_at, 2 * total_rows + window)
    key_pos = jnp.concatenate([cache_at, fresh_at])[None, :]
    query_pos = token_at[:, None]
    weighted, stats = attend_forward(q_low, keys, values, query_pos, key_pos, window)
    row_max = stats[:, :heads].T
    row_sum = stats[:, HD // 2 : HD // 2 + heads].T
    all_lse = blk_all(row_max + jnp.log(row_sum))
    top = jnp.max(all_lse, axis=0)
    lse = top + jnp.log(jnp.sum(jnp.exp(all_lse - top[None]), axis=0))
    share = jnp.exp(row_max - lse).T
    att_part = weighted.reshape(total_rows, heads, HD) * share[:, :, None]
    att_low = att_part.reshape(total_rows, width).astype(BF)
    rows_two = rows_one + valid * scatter_rows(matmul(att_low, out_full), True)

    rows_out, kept_two = ffn_forward(rows_two, gains[3], ffn2_gate_up, ffn2_down, valid)
    block_output = by_order(first, rows_out, mp_swap(rows_out)).reshape(tok_rows, model)

    grad_rows, gain_four, grad_gate_up_two, grad_down_two = ffn_backward(
        grad_rows, kept_two, gains[3], ffn2_gate_up, ffn2_down, valid
    )

    branch_a = gather_rows((valid * grad_rows).astype(BF), True)
    grad_att = matmul_nt(branch_a, out_full).astype(BF)
    delta_part = jnp.sum(
        (grad_att.astype(F32) * att_low.astype(F32)).reshape(total_rows, heads, HD), axis=-1
    )
    delta = jnp.sum(blk_all(delta_part.T), axis=0)
    gap = jnp.zeros((total_rows, HD // 2 - heads), F32)
    stats_b = jnp.concatenate([lse.T, gap, delta.T, gap], axis=1)
    grad_q, grad_keys, grad_values = attend_backward(
        q_low, keys, values, grad_att, stats_b, query_pos, key_pos, window
    )
    grad_q_low = rotate(grad_q, cosine, sine, -1.0).astype(BF)
    grad_k_low = rotate(
        grad_keys[cache_rows:], own_block(cosine), own_block(sine), -1.0
    ).astype(BF)
    grad_v_low = grad_values[cache_rows:].astype(BF)
    kv_cache_grad = jnp.stack([grad_keys[:cache_rows], grad_values[:cache_rows]])[None]
    grad_normed = matmul_nt(grad_q_low, qkv_full[0])
    grad_fresh = matmul_nt(grad_k_low, qkv_full[1]) + matmul_nt(grad_v_low, qkv_full[2])
    grad_normed = lax.dynamic_update_slice_in_dim(
        grad_normed, own_block(grad_normed) + grad_fresh, first_pos, 0
    )
    grad_in, gain_three = norm_backward(
        scatter_rows(grad_normed, True), unit_a, inverse_a, gains[2]
    )
    grad_rows = grad_rows + grad_in
    shard_cols = model // blocks

    def own_cols(array):
        return lax.dynamic_slice_in_dim(array, dev_index * shard_cols, shard_cols, 1)

    att_all = blk_gather_rows(blk_scatter(att_low, 0).astype(BF))
    grad_attn_out = matmul_tn(att_all, own_cols(branch_a))
    grad_q_own = blk_scatter(grad_q_low, 0).astype(BF)
    grad_qkv_all = blk_gather_rows(jnp.concatenate([grad_q_own, grad_k_low, grad_v_low], axis=1))
    normed_cols = own_cols(full_a)
    grad_qkv = jnp.concatenate(
        [matmul_tn(normed_cols, grad_qkv_all[:, k * width : (k + 1) * width]) for k in range(3)],
        axis=0,
    )

    grad_rows, gain_two, grad_gate_up_one, grad_down_one = ffn_backward(
        grad_rows, kept_one, gains[1], ffn1_gate_up, ffn1_down, valid
    )

    branch_m = gather_rows((valid * grad_rows).astype(BF), True)
    grad_mamba_out = matmul_tn(gated, branch_m)
    grad_gated = matmul_nt(branch_m, mamba_out)
    grad_mixed = grad_gated * jax.nn.silu(z_lin)
    grad_z = (grad_gated * mixed * silu_slope(z_lin)).astype(BF)
    grad_skip = jnp.sum(grad_mixed * conv_out, axis=0)
    grad_u, grad_step, grad_in_l, grad_out_l, grad_decay, grad_state = scan_backward(
        step, drive, grad_mixed, in_b, out_b, before, decay
    )
    grad_step = grad_step + grad_u * conv_out
    grad_dt = (grad_step * valid_all * jax.nn.sigmoid(dt_lin)).astype(BF)
    grad_dt_bias = jnp.sum(grad_dt.astype(F32), axis=0)
    grad_dt_proj = matmul_tn(dt_low, grad_dt)
    grad_proj = sum_small(
        jnp.concatenate(
            [matmul_nt(grad_dt, dt_proj), jnp.sum(grad_in_l, axis=-1), jnp.sum(grad_out_l, axis=-1)],
            axis=1,
        )
    ).astype(BF)
    grad_x_proj = matmul_tn(grad_proj, conv_low)
    grad_conv = grad_u * step + grad_mixed * skip + matmul(grad_proj, x_proj)
    grad_pre = grad_conv * silu_slope(conv_pre)
    grad_conv_b = jnp.sum(grad_pre, axis=0)
    grad_conv_w = jnp.stack(
        [jnp.sum(grad_pre * padded_f[k : k + total_rows], axis=0) for k in range(taps)]
    )
    grad_padded = sum(
        (
            jnp.pad(conv_w[k] * grad_pre, ((k, taps - 1 - k), (0, 0)))
            for k in range(taps)
        )
    )
    grad_x = grad_padded[taps - 1 :].astype(BF)
    grad_w_in = jnp.concatenate([matmul_tn(full_m, grad_x), matmul_tn(full_m, grad_z)], axis=0)
    grad_normed = scatter_rows(matmul_nt(grad_x, w_in[0]) + matmul_nt(grad_z, w_in[1]), True)
    grad_in, gain_one = norm_backward(grad_normed, unit_m, inverse_m, gains[0])
    grad_rows = grad_rows + grad_in
    input_grad = by_order(first, grad_rows, mp_swap(grad_rows)).reshape(tok_rows, model)

    fresh_kv = jnp.stack([k_low, v_low])
    if direct() and cache_rows >= total_rows:
        following = from_ahead(kv_cache[0, :, :total_rows], 1)
        following = jnp.where(dev_index == blocks - 1, fresh_kv, following)
        both = jnp.concatenate([kv_cache[0], following], axis=1)
        new_cache = lax.dynamic_slice_in_dim(both, seq_len, cache_rows, 1)
    else:
        cache_full = lax.all_gather(kv_cache[0], "blk", axis=1, tiled=True)
        both = jnp.concatenate([cache_full, fresh_kv], axis=1)
        new_cache = lax.dynamic_slice_in_dim(both, seq_len + dev_index * cache_rows, cache_rows, 1)

    gain_part = jnp.stack([gain_one, gain_two, gain_three, gain_four])
    gain_own = blk_scatter(gain_part, 1)
    gain_own = gain_own + mp_swap(gain_own)
    small = [
        (grad_x_proj, x_proj.shape),
        (grad_dt_proj, dt_proj.shape),
        (grad_decay * decay, a_log.shape),
        (grad_conv_w, conv_weight.shape),
        (gain_own, norm_gains.shape),
        (grad_conv_b[None], conv_bias.shape),
        (grad_dt_bias[None], dt_bias.shape),
        (grad_skip[None], d_skip.shape),
    ]
    packed = jnp.concatenate([piece for piece, _ in small], axis=0)
    packed = jnp.pad(packed, ((0, -packed.shape[0] % 64), (0, 0)))
    packed = seq_sum(packed)
    summed = []
    begin = 0
    for piece, shape in small:
        summed.append(packed[begin : begin + piece.shape[0]].reshape(shape))
        begin += piece.shape[0]
    sum_x_proj, sum_dt_proj, sum_a_log, sum_conv_w, sum_gains, sum_conv_b, sum_dt_bias, sum_skip = (
        summed
    )
    return (
        block_output,
        input_grad,
        final_state.astype(BF)[None],
        new_conv[None],
        new_cache[None],
        grad_state[None],
        grad_padded[: taps - 1][None],
        kv_cache_grad,
        sum_gains,
        seq_sum(grad_w_in).reshape(w_in.shape),
        sum_conv_w,
        sum_conv_b,
        sum_x_proj,
        sum_dt_proj,
        sum_dt_bias,
        sum_a_log,
        sum_skip,
        seq_sum(grad_mamba_out),
        seq_sum(grad_gate_up_one).reshape(ffn1_gate_up.shape),
        seq_sum(grad_down_one),
        seq_sum(grad_qkv).reshape(qkv_proj.shape),
        seq_sum(grad_attn_out),
        seq_sum(grad_gate_up_two).reshape(ffn2_gate_up.shape),
        seq_sum(grad_down_two),
    )


def solution(mesh):
    both = ("blk", "mp")
    return jax.shard_map(
        shards,
        mesh=mesh,
        in_specs=(
            P(("seqs", "blk"), None),
            P(("seqs", "blk"), None),
            P("seqs"),
            P("seqs"),
            P("seqs", None, both),
            P("seqs", None, both),
            P("seqs", None, "blk", "mp"),
            P(None, "blk"),
            P(None, None, both),
            P(None, both),
            P(both),
            P(None, both),
            P(None, both),
            P(both),
            P(None, both),
            P(both),
            P(both, None),
            P(None, None, both),
            P(both, None),
            P(None, "blk", "mp"),
            P("mp", "blk"),
            P(None, None, both),
            P(both, None),
        ),
        out_specs=(
            P(("seqs", "blk"), None),
            P(("seqs", "blk"), None),
            P("seqs", None, both),
            P("seqs", None, both),
            P("seqs", None, "blk", "mp"),
            P("seqs", None, both),
            P("seqs", None, both),
            P("seqs", None, "blk", "mp"),
            P(None, "blk"),
            P(None, None, both),
            P(None, both),
            P(both),
            P(None, both),
            P(None, both),
            P(both),
            P(None, both),
            P(both),
            P(both, None),
            P(None, None, both),
            P(both, None),
            P(None, "blk", "mp"),
            P("mp", "blk"),
            P(None, None, both),
            P(both, None),
        ),
        check_vma=False,
    )
```

time: 3880 us -> 1160 us (0.30)
  waiting for transfers between devices: 2650 us -> 507 us
  local copies, waits for them, and re-layouts: 456 us -> 98.5 us
  starting transfers between devices: 48.3 us -> 297 us
  blocking collectives: 232 us -> 0 us
  other arithmetic: 292 us -> 108 us
  matrix products: 153 us -> 75.1 us
  Pallas kernels: 0 us -> 46.4 us
    reduce_scatter x8 -> x0, waiting for transfers between devices: 1040 us -> none  [the longest x1 215 us: shards(): lax.psum_scatter(grad_gate_up_one.astype(jnp.bfloat16), 'blk', scatter_di...]
    all_gather x9 -> x2, waiting for transfers between devices: 863 us -> 0.01 us  [the longest x1 0.01 us: shards(): qkv_full = lax.all_gather(qkv_proj, 'blk', axis=1, tiled=True)]
    ppermute x14 -> x198, waiting for transfers between devices: 106 us -> 507 us  [the longest x72 198 us: exchange(): return lax.ppermute(array, 'seqs', pairs[way])]
    psum x8 -> x0, waiting for transfers between devices: 387 us -> none  [the longest x1 292 us: shards(): lax.psum(red_w_in.astype(jnp.bfloat16), 'seqs').astype(jnp.float32)]
    ppermute x14 -> x198, starting transfers between devices: 45.2 us -> 297 us  [the longest x46 155 us: from_ahead(): lax.ppermute(value, 'blk', [((i + steps) % count, i) for i in range(count)])]
    unnamed x47 -> x2, waiting for transfers between devices: 250 us -> 0.7 us
    all_gather x10 -> x0, blocking collectives: 192 us -> none  [the longest x1 29.4 us: shards(): lax.all_gather(d_skip, 'blk', axis=0, tiled=True)]
    pad x114 -> x0, local copies, waits for them, and re-layouts: 155 us -> none  [scan_piece(): lax.associative_scan(pair_combine, (shrink[:, -1], inner_state[:, -1]))]
  transfers between devices with their start and end apart: 50 -> 200, of which waited for: 43 -> 85; matrix products, arithmetic and copies ran while one was open for 9% -> 22% of each run, Pallas kernels for 0% -> 4%
where the time goes in v1:
time: 1160 us; the launch traced here: 1150 us
  waiting for transfers between devices  507 us (44%)
  starting transfers between devices  297 us (26%)
  other arithmetic  108 us (9%)
  local copies, waits for them, and re-layouts  98.5 us (8%)
  matrix products  75.1 us (6%)
  Pallas kernels  46.4 us (4%)
  between operations  19.8 us (2%)
    ppermute x72, waiting for transfers between devices, exchange(): return lax.ppermute(array, 'seqs', pairs[way])  198 us
    ppermute x46, starting transfers between devices, from_ahead(): lax.ppermute(value, 'blk', [((i + steps) % count, i) for i in range(count)])  155 us
    ppermute x46, waiting for transfers between devices, from_ahead(): lax.ppermute(value, 'blk', [((i + steps) % count, i) for i in range(count)])  154 us
    ppermute x33, waiting for transfers between devices, to_ahead(): lax.ppermute(value, 'blk', [(i, (i + steps) % count) for i in range(count)])  148 us
    ppermute x72, starting transfers between devices, exchange(): return lax.ppermute(array, 'seqs', pairs[way])  68.4 us
    ppermute x33, starting transfers between devices, to_ahead(): lax.ppermute(value, 'blk', [(i, (i + steps) % count) for i in range(count)])  66.9 us
    dot_general x15, matrix products, matmul(): return jnp.dot(left_op, right_op, preferred_element_type=F32)  32.5 us
    unnamed x288, local copies, waits for them, and re-layouts  31.4 us
  transfers between devices with their start and end apart: 200, of which 85 were waited for; matrix products, arithmetic and copies ran while one was open for 22% of the time, Pallas kernels for 4%

profile of v1, /device:TPU:0, one launch (start us, length us, event | category | flops | bytes accessed | tf_op | source)
XLA Modules:
  0.0 1152.5 jit_solution(4070174384380004638)
XLA Ops:
  31.1 12.9 %collective-permute-done.4 = bf16[64,1536]{1,0:T(8,128)(2,1)S(1)} collective-permute-done((bf16[64,1536]{1,0:T(8,128)(2,1)}, bf16[64,1536]{1,0:T(8,128)(2,1)S(1)}, u32[]{:S(2)}, u32[]{:S(2)}) %collective-permute-start.4) | collective-permute-done | bytes 196640 | tf_op jit(solution)/shard_map/ppermute | solution.py:35
  56.9 17.1 %collective-permute-start.13 = (bf16[256,128]{1,0:T(8,128)(2,1)S(1)}, bf16[256,128]{1,0:T(8,128)(2,1)S(1)}, u32[]{:S(2)}, u32[]{:S(2)}) collective-permute-start(bf16[256,128]{1,0:T(8,128)(2,1)S(1)} %fusion.127), channel_id=1, source_target_pairs={{6,0},{0,2},{2,4},{4,6},{7,1},{1,3},{3,5},{5,7},{14,8},{8,10},{10,... | collective-permute-start | bytes 196616 | tf_op jit(solution)/shard_map/ppermute | solution.py:35
  92.4 11.2 scan_fwd.1
  128.4 14.9 %collective-permute-done.18 = bf16[64,1536]{1,0:T(8,128)(2,1)S(1)} collective-permute-done((bf16[64,1536]{1,0:T(8,128)(2,1)S(1)}, bf16[64,1536]{1,0:T(8,128)(2,1)S(1)}, u32[]{:S(2)}, u32[]{:S(2)}) %collective-permute-start.18) | collective-permute-done | bytes 196640 | tf_op jit(solution)/shard_map/ppermute | solution.py:40
  143.4 17.4 %collective-permute-start.58 = (bf16[64,1536]{1,0:T(8,128)(2,1)}, bf16[64,1536]{1,0:T(8,128)(2,1)}, u32[]{:S(2)}, u32[]{:S(2)}) collective-permute-start(bf16[64,1536]{1,0:T(8,128)(2,1)} %get-tuple-element.210), channel_id=1, source_target_pairs={{6,0},{0,2},{2,4},{4,6},{7,1},{1,3},{3,5},{5,7},{14,8},{8,10},{10,... | collective-permute-start | bytes 589832 | tf_op jit(solution)/shard_map/ppermute | solution.py:35
  160.8 15.4 %collective-permute-done.17 = bf16[64,1536]{1,0:T(8,128)(2,1)S(1)} collective-permute-done((bf16[64,1536]{1,0:T(8,128)(2,1)S(1)}, bf16[64,1536]{1,0:T(8,128)(2,1)S(1)}, u32[]{:S(2)}, u32[]{:S(2)}) %collective-permute-start.17) | collective-permute-done | bytes 196640 | tf_op jit(solution)/shard_map/ppermute | solution.py:40
  179.7 16.1 %collective-permute-done.19 = bf16[64,1536]{1,0:T(8,128)(2,1)S(1)} collective-permute-done((bf16[64,1536]{1,0:T(8,128)(2,1)S(1)}, bf16[64,1536]{1,0:T(8,128)(2,1)S(1)}, u32[]{:S(2)}, u32[]{:S(2)}) %collective-permute-start.19) | collective-permute-done | bytes 196640 | tf_op jit(solution)/shard_map/ppermute | solution.py:35
  196.5 11.2 collective-permute-done.20
  208.3 12.8 %collective-permute-done.21 = bf16[64,1536]{1,0:T(8,128)(2,1)S(1)} collective-permute-done((bf16[64,1536]{1,0:T(8,128)(2,1)S(1)}, bf16[64,1536]{1,0:T(8,128)(2,1)S(1)}, u32[]{:S(2)}, u32[]{:S(2)}) %collective-permute-start.21) | collective-permute-done | bytes 196640 | tf_op jit(solution)/shard_map/ppermute | solution.py:35
  247.4 41.7 %collective-permute-done.29 = bf16[64,1536]{1,0:T(8,128)(2,1)S(1)} collective-permute-done((bf16[64,1536]{1,0:T(8,128)(2,1)S(1)}, bf16[64,1536]{1,0:T(8,128)(2,1)S(1)}, u32[]{:S(2)}, u32[]{:S(2)}) %collective-permute-start.29) | collective-permute-done | bytes 196640 | tf_op jit(solution)/shard_map/ppermute | solution.py:40
  377.8 10.8 collective-permute-done.38
  442.4 13.3 %collective-permute-start.171 = (bf16[128,768]{1,0:T(8,128)(2,1)S(1)}, bf16[128,768]{1,0:T(8,128)(2,1)S(1)}, u32[]{:S(2)}, u32[]{:S(2)}) collective-permute-start(bf16[128,768]{1,0:T(8,128)(2,1)S(1)} %add_convert_fusion.1), channel_id=1, source_target_pairs={{6,0},{0,2},{2,4},{4,6},{7,1},{1,3},{3,5},{5,7},{14,8},{8,10},{10,... | collective-permute-start | bytes 589832 | tf_op jit(solution)/shard_map/ppermute | solution.py:35
  458.1 9.3 collective-permute-done.42
  480.6 12.5 %collective-permute-start.46 = (bf16[64,1536]{1,0:T(8,128)(2,1)S(1)}, bf16[64,1536]{1,0:T(8,128)(2,1)S(1)}, u32[]{:S(2)}, u32[]{:S(2)}) collective-permute-start(bf16[64,1536]{1,0:T(8,128)(2,1)S(1)} %get-tuple-element.212), channel_id=1, source_target_pairs={{6,0},{0,2},{2,4},{4,6},{7,1},{1,3},{3,5},{5,7},{14,8},{8,10},{10,... | collective-permute-start | bytes 589832 | tf_op jit(solution)/shard_map/ppermute | solution.py:35
  528.8 15.9 %collective-permute-done.190 = bf16[128,1536]{1,0:T(8,128)(2,1)S(1)} collective-permute-done((bf16[128,1536]{1,0:T(8,128)(2,1)S(1)}, bf16[128,1536]{1,0:T(8,128)(2,1)S(1)}, u32[]{:S(2)}, u32[]{:S(2)}) %collective-permute-start.190) | collective-permute-done | bytes 393248 | tf_op jit(solution)/shard_map/ppermute | solution.py:168
  636.4 10.3 collective-permute-done.75
  648.9 10.8 attend_bwd.1
  738.9 16.2 %collective-permute-done.158 = bf16[128,2304]{1,0:T(8,128)(2,1)S(1)} collective-permute-done((bf16[128,2304]{1,0:T(8,128)(2,1)S(1)}, bf16[128,2304]{1,0:T(8,128)(2,1)S(1)}, u32[]{:S(2)}, u32[]{:S(2)}) %collective-permute-start.158) | collective-permute-done | bytes 589856 | tf_op jit(solution)/shard_map/ppermute | solution.py:35
  762.1 13.2 %collective-permute-start.80 = (bf16[64,1536]{1,0:T(8,128)(2,1)S(1)}, bf16[64,1536]{1,0:T(8,128)(2,1)S(1)}, u32[]{:S(2)}, u32[]{:S(2)}) collective-permute-start(bf16[64,1536]{1,0:T(8,128)(2,1)S(1)} %get-tuple-element.337), channel_id=1, source_target_pairs={{0,2},{2,4},{4,6},{6,0},{1,3},{3,5},{5,7},{7,1},{8,10},{10,12},{12... | collective-permute-start | bytes 589832 | tf_op jit(solution)/shard_map/ppermute | solution.py:40
  800.3 12.6 %collective-permute-done.82 = bf16[64,1536]{1,0:T(8,128)(2,1)S(1)} collective-permute-done((bf16[64,1536]{1,0:T(8,128)(2,1)S(1)}, bf16[64,1536]{1,0:T(8,128)(2,1)S(1)}, u32[]{:S(2)}, u32[]{:S(2)}) %collective-permute-start.82) | collective-permute-done | bytes 196640 | tf_op jit(solution)/shard_map/ppermute | solution.py:35
  828.8 20.9 %collective-permute-done.166 = bf16[144,768]{1,0:T(8,128)(2,1)S(1)} collective-permute-done((bf16[144,768]{1,0:T(8,128)(2,1)S(1)}, bf16[144,768]{1,0:T(8,128)(2,1)S(1)}, u32[]{:S(2)}, u32[]{:S(2)}) %collective-permute-start.166) | collective-permute-done | bytes 221216 | tf_op jit(solution)/shard_map/ppermute | solution.py:168
  940.5 16.5 %scan_bwd.1 = (f32[512,384]{1,0:T(8,128)}, f32[512,384]{1,0:T(8,128)}, f32[512,16,128]{2,1,0:T(8,128)}, f32[512,16,128]{2,1,0:T(8,128)}, f32[16,384]{1,0:T(8,128)}, /*index=5*/f32[16,384]{1,0:T(8,128)}) custom-call(f32[512,384]{1,0:T(8,128)} %get-tuple-element.234.step_ref, f32[512,384]{1,0:T(8,128)} %get-tuple-element.233.u_ref, ...), custom_call_target="tpu_custom_call" | custom-call | tf_op jit(solution)/shard_map/scan_bwd/pallas_call | solution.py:367
  1042.6 10.2 collective-permute-done.136
  1131.4 10.9 collective-permute-done.125
  (1096 shorter events, 778.8 us)
Async XLA Ops:
  7.2 317.0 %all-gather.3.cloned.1.call-start = ((), (), s32[]{:S(2)}) async-start(), calls=%async_computation | async-start | bytes 8847360 | tf_op jit(solution)/shard_map/all_gather | solution.py:552
  8.0 402.4 %all-gather.5.cloned.1.call-start = ((), (), s32[]{:S(2)}) async-start(), calls=%async_computation.1 | async-start | bytes 2949120 | tf_op jit(solution)/shard_map/all_gather | solution.py:553
  112.1 125.4 %collective-permute-start.56 = (bf16[64,1536]{1,0:T(8,128)(2,1)}, bf16[64,1536]{1,0:T(8,128)(2,1)}, u32[]{:S(2)}, u32[]{:S(2)}) collective-permute-start(bf16[64,1536]{1,0:T(8,128)(2,1)} %get-tuple-element.210), channel_id=1, source_target_pairs={{2,0},{4,2},{6,4},{0,6},{3,1},{5,3},{7,5},{1,7},{10,8},{12,10},{14... | collective-permute-start | bytes 589832 | tf_op jit(solution)/shard_map/ppermute | solution.py:35
  116.3 123.4 %collective-permute-start.57 = (bf16[64,1536]{1,0:T(8,128)(2,1)}, bf16[64,1536]{1,0:T(8,128)(2,1)}, u32[]{:S(2)}, u32[]{:S(2)}) collective-permute-start(bf16[64,1536]{1,0:T(8,128)(2,1)} %get-tuple-element.210), channel_id=1, source_target_pairs={{4,0},{6,2},{0,4},{2,6},{5,1},{7,3},{1,5},{3,7},{12,8},{14,10},{8,... | collective-permute-start | bytes 589832 | tf_op jit(solution)/shard_map/ppermute | solution.py:35
  121.9 54.2 %collective-permute-start.17 = (bf16[64,1536]{1,0:T(8,128)(2,1)S(1)}, bf16[64,1536]{1,0:T(8,128)(2,1)S(1)}, u32[]{:S(2)}, u32[]{:S(2)}) collective-permute-start(bf16[64,1536]{1,0:T(8,128)(2,1)S(1)} %get-tuple-element.355), channel_id=1, source_target_pairs={{0,4},{2,6},{4,0},{6,2},{1,5},{3,7},{5,1},{7,3},{8,12},{10,14},{12... | collective-permute-start | bytes 589832 | tf_op jit(solution)/shard_map/ppermute | solution.py:40
  143.4 97.4 %collective-permute-start.58 = (bf16[64,1536]{1,0:T(8,128)(2,1)}, bf16[64,1536]{1,0:T(8,128)(2,1)}, u32[]{:S(2)}, u32[]{:S(2)}) collective-permute-start(bf16[64,1536]{1,0:T(8,128)(2,1)} %get-tuple-element.210), channel_id=1, source_target_pairs={{6,0},{0,2},{2,4},{4,6},{7,1},{1,3},{3,5},{5,7},{14,8},{8,10},{10,... | collective-permute-start | bytes 589832 | tf_op jit(solution)/shard_map/ppermute | solution.py:35
  176.1 66.1 %collective-permute-start.59 = (bf16[64,1536]{1,0:T(8,128)(2,1)}, bf16[64,1536]{1,0:T(8,128)(2,1)}, u32[]{:S(2)}, u32[]{:S(2)}) collective-permute-start(bf16[64,1536]{1,0:T(8,128)(2,1)} %get-tuple-element.210), channel_id=1, source_target_pairs={{0,1},{1,0},{2,3},{3,2},{4,5},{5,4},{6,7},{7,6},{8,9},{9,8},{10,11... | collective-permute-start | bytes 589832 | tf_op jit(solution)/shard_map/ppermute | solution.py:44
  226.9 190.7 %collective-permute-start.109 = (bf16[2,512,768]{2,1,0:T(8,128)(2,1)}, bf16[2,512,768]{2,1,0:T(8,128)(2,1)}, u32[]{:S(2)}, u32[]{:S(2)}) collective-permute-start(bf16[2,512,768]{2,1,0:T(8,128)(2,1)} %bitcast.111), channel_id=1, source_target_pairs={{2,0},{4,2},{6,4},{0,6},{3,1},{5,3},{7,5},{1,7},{10,8},{12,10},{14... | collective-permute-start | bytes 4718600 | tf_op jit(solution)/shard_map/ppermute | solution.py:35
  240.7 61.9 %collective-permute-start.61 = (bf16[64,1536]{1,0:T(8,128)(2,1)}, bf16[64,1536]{1,0:T(8,128)(2,1)S(1)}, u32[]{:S(2)}, u32[]{:S(2)}) collective-permute-start(bf16[64,1536]{1,0:T(8,128)(2,1)} %collective-permute-done.57), channel_id=1, source_target_pairs={{0,1},{1,0},{2,3},{3,2},{4,5},{5,4},{6,7},{7,6},{8,9},{9,8},{10,11... | collective-permute-start | bytes 589832 | tf_op jit(solution)/shard_map/ppermute | solution.py:44
  243.5 53.2 %collective-permute-start.28 = (bf16[64,1536]{1,0:T(8,128)(2,1)S(1)}, bf16[64,1536]{1,0:T(8,128)(2,1)S(1)}, u32[]{:S(2)}, u32[]{:S(2)}) collective-permute-start(bf16[64,1536]{1,0:T(8,128)(2,1)S(1)} %get-tuple-element.352), channel_id=1, source_target_pairs={{0,4},{2,6},{4,0},{6,2},{1,5},{3,7},{5,1},{7,3},{8,12},{10,14},{12... | collective-permute-start | bytes 589832 | tf_op jit(solution)/shard_map/ppermute | solution.py:40
  611.5 86.0 %collective-permute-start.188 = (bf16[384,512]{1,0:T(8,128)(2,1)}, bf16[384,512]{1,0:T(8,128)(2,1)}, u32[]{:S(2)}, u32[]{:S(2)}) collective-permute-start(bf16[384,512]{1,0:T(8,128)(2,1)} %fusion.83), channel_id=1, source_target_pairs={{0,8},{8,0},{16,24},{24,16},{1,9},{9,1},{17,25},{25,17},{2,10},{10... | collective-permute-start | bytes 1179656 | tf_op jit(solution)/shard_map/ppermute | solution.py:168
  613.4 87.7 %collective-permute-start.184 = (bf16[384,512]{1,0:T(8,128)(2,1)}, bf16[384,512]{1,0:T(8,128)(2,1)}, u32[]{:S(2)}, u32[]{:S(2)}) collective-permute-start(bf16[384,512]{1,0:T(8,128)(2,1)} %fusion.84), channel_id=1, source_target_pairs={{0,16},{16,0},{8,24},{24,8},{1,17},{17,1},{9,25},{25,9},{2,18},{18... | collective-permute-start | bytes 1179656 | tf_op jit(solution)/shard_map/ppermute | solution.py:168
  636.3 53.4 %collective-permute-start.178 = (bf16[192,384]{1,0:T(8,128)(2,1)}, bf16[192,384]{1,0:T(8,128)(2,1)}, u32[]{:S(2)}, u32[]{:S(2)}) collective-permute-start(bf16[192,384]{1,0:T(8,128)(2,1)} %dynamic-slice_bitcast_fusion.42), channel_id=1, source_target_pairs={{0,16},{16,0},{8,24},{24,8},{1,17},{17,1},{9,25},{25,9},{2,18},{18... | collective-permute-start | bytes 442376 | tf_op jit(solution)/shard_map/ppermute | solution.py:168
  678.9 83.0 %collective-permute-start.77 = (bf16[4,64,1536]{2,1,0:T(8,128)(2,1)}, bf16[4,64,1536]{2,1,0:T(8,128)(2,1)S(1)}, u32[]{:S(2)}, u32[]{:S(2)}) collective-permute-start(bf16[4,64,1536]{2,1,0:T(8,128)(2,1)} %dynamic-slice_bitcast_fusion.5), channel_id=1, source_target_pairs={{0,1},{1,0},{2,3},{3,2},{4,5},{5,4},{6,7},{7,6},{8,9},{9,8},{10,11... | collective-permute-start | bytes 2359304 | tf_op jit(solution)/shard_map/ppermute | solution.py:44
  761.2 53.5 %collective-permute-start.160 = (bf16[288,768]{1,0:T(8,128)(2,1)S(1)}, bf16[288,768]{1,0:T(8,128)(2,1)S(1)}, u32[]{:S(2)}, u32[]{:S(2)}) collective-permute-start(bf16[288,768]{1,0:T(8,128)(2,1)S(1)} %dynamic-slice_bitcast_fusion.11), channel_id=1, source_target_pairs={{0,8},{8,0},{16,24},{24,16},{1,9},{9,1},{17,25},{25,17},{2,10},{10... | collective-permute-start | bytes 1327112 | tf_op jit(solution)/shard_map/ppermute | solution.py:168
  824.0 74.5 %collective-permute-start.88 = (bf16[4,64,1536]{2,1,0:T(8,128)(2,1)S(1)}, bf16[4,64,1536]{2,1,0:T(8,128)(2,1)S(1)}, u32[]{:S(2)}, u32[]{:S(2)}) collective-permute-start(bf16[4,64,1536]{2,1,0:T(8,128)(2,1)S(1)} %bitcast.957), channel_id=1, source_target_pairs={{0,1},{1,0},{2,3},{3,2},{4,5},{5,4},{6,7},{7,6},{8,9},{9,8},{10,11... | collective-permute-start | bytes 2359304 | tf_op jit(solution)/shard_map/ppermute | solution.py:44
  824.1 74.6 %collective-permute-start.142 = (bf16[768,512]{1,0:T(8,128)(2,1)S(1)}, bf16[768,512]{1,0:T(8,128)(2,1)S(1)}, u32[]{:S(2)}, u32[]{:S(2)}) collective-permute-start(bf16[768,512]{1,0:T(8,128)(2,1)S(1)} %dynamic-slice_bitcast_fusion.2), channel_id=1, source_target_pairs={{0,16},{16,0},{8,24},{24,8},{1,17},{17,1},{9,25},{25,9},{2,18},{18... | collective-permute-start | bytes 2359304 | tf_op jit(solution)/shard_map/ppermute | solution.py:168
  825.7 74.6 %collective-permute-start.138 = (bf16[768,512]{1,0:T(8,128)(2,1)S(1)}, bf16[768,512]{1,0:T(8,128)(2,1)S(1)}, u32[]{:S(2)}, u32[]{:S(2)}) collective-permute-start(bf16[768,512]{1,0:T(8,128)(2,1)S(1)} %dynamic-slice_bitcast_fusion.3), channel_id=1, source_target_pairs={{0,8},{8,0},{16,24},{24,16},{1,9},{9,1},{17,25},{25,17},{2,10},{10... | collective-permute-start | bytes 2359304 | tf_op jit(solution)/shard_map/ppermute | solution.py:168
  931.1 55.4 %collective-permute-start.144 = (bf16[384,512]{1,0:T(8,128)(2,1)S(1)}, bf16[384,512]{1,0:T(8,128)(2,1)}, u32[]{:S(2)}, u32[]{:S(2)}) collective-permute-start(bf16[384,512]{1,0:T(8,128)(2,1)S(1)} %fusion.87), channel_id=1, source_target_pairs={{0,8},{8,0},{16,24},{24,16},{1,9},{9,1},{17,25},{25,17},{2,10},{10... | collective-permute-start | bytes 1179656 | tf_op jit(solution)/shard_map/ppermute | solution.py:168
  933.1 54.6 %collective-permute-start.140 = (bf16[384,512]{1,0:T(8,128)(2,1)S(1)}, bf16[384,512]{1,0:T(8,128)(2,1)}, u32[]{:S(2)}, u32[]{:S(2)}) collective-permute-start(bf16[384,512]{1,0:T(8,128)(2,1)S(1)} %fusion.88), channel_id=1, source_target_pairs={{0,16},{16,0},{8,24},{24,8},{1,17},{17,1},{9,25},{25,9},{2,18},{18... | collective-permute-start | bytes 1179656 | tf_op jit(solution)/shard_map/ppermute | solution.py:168
  983.3 57.0 %collective-permute-start.126 = (bf16[768,384]{1,0:T(8,128)(2,1)S(1)}, bf16[768,384]{1,0:T(8,128)(2,1)S(1)}, u32[]{:S(2)}, u32[]{:S(2)}) collective-permute-start(bf16[768,384]{1,0:T(8,128)(2,1)S(1)} %dynamic-slice_bitcast_fusion.8), channel_id=1, source_target_pairs={{0,16},{16,0},{8,24},{24,8},{1,17},{17,1},{9,25},{25,9},{2,18},{18... | collective-permute-start | bytes 1769480 | tf_op jit(solution)/shard_map/ppermute | solution.py:168
  987.8 88.6 %collective-permute-start.145 = (bf16[768,512]{1,0:T(8,128)(2,1)S(1)}, bf16[768,512]{1,0:T(8,128)(2,1)S(1)}, u32[]{:S(2)}, u32[]{:S(2)}) collective-permute-start(bf16[768,512]{1,0:T(8,128)(2,1)S(1)} %bitcast.876), channel_id=1, source_target_pairs={{0,16},{16,0},{8,24},{24,8},{1,17},{17,1},{9,25},{25,9},{2,18},{18... | collective-permute-start | bytes 2359304 | tf_op jit(solution)/shard_map/ppermute | solution.py:168
  990.3 86.3 %collective-permute-start.141 = (bf16[768,512]{1,0:T(8,128)(2,1)S(1)}, bf16[768,512]{1,0:T(8,128)(2,1)S(1)}, u32[]{:S(2)}, u32[]{:S(2)}) collective-permute-start(bf16[768,512]{1,0:T(8,128)(2,1)S(1)} %bitcast.877), channel_id=1, source_target_pairs={{0,8},{8,0},{16,24},{24,16},{1,9},{9,1},{17,25},{25,17},{2,10},{10... | collective-permute-start | bytes 2359304 | tf_op jit(solution)/shard_map/ppermute | solution.py:168
  1012.5 64.2 %collective-permute-start.104 = (bf16[4,64,1536]{2,1,0:T(8,128)(2,1)S(1)}, bf16[4,64,1536]{2,1,0:T(8,128)(2,1)S(1)}, u32[]{:S(2)}, u32[]{:S(2)}) collective-permute-start(bf16[4,64,1536]{2,1,0:T(8,128)(2,1)S(1)} %dynamic-slice_bitcast_fusion.4), channel_id=1, source_target_pairs={{0,1},{1,0},{2,3},{3,2},{4,5},{5,4},{6,7},{7,6},{8,9},{9,8},{10,11... | collective-permute-start | bytes 2359304 | tf_op jit(solution)/shard_map/ppermute | solution.py:44
  (305 other events, 4338.6 us)
Sparse Core Ops, SparseCore 0:
  9.6 185.0 all-gather.2
  196.3 66.4 all-gather.4
